TPU v7x, 32 devices: a whole 2x2x4 slice. The times are simulated.
32 devices in a mesh: dp: 8 (over y, x, core), chan: 4 (over z).
Axes of the slice: x: 2, y: 2, z: 4, core: 2. Of those that a mesh axis runs over, the one named last changes fastest.
Arguments:
- inputs: bfloat16 [192, 152, 800], P('dp', None, 'chan'), may hold values from -6 to 6
- ocean_mask: int32 [192, 152], P('dp'), may hold values 0 or 1
- counts: int32 [4], replicated, may hold values from 1 to 2
- kernel: float32 [7, 7, 800], P(None, None, 'chan'), may hold values from -0.875 to 0.875
- conv_bias: float32 [800], P('chan'), may hold values from -3 to 3
- norm_gain: float32 [800], P('chan'), may hold values from 0.5 to 1.5
- norm_bias: float32 [800], P('chan'), may hold values from -3 to 3
- weight_in: bfloat16 [800, 3200], P(None, 'chan'), may hold values from -0.21875 to 0.21875
- bias_in: float32 [3200], P('chan'), may hold values from -3 to 3
- weight_out: bfloat16 [3200, 800], P('chan'), may hold values from -0.21875 to 0.21875
- bias_out: float32 [800], P('chan'), may hold values from -3 to 3
- cotangent: bfloat16 [192, 152, 800], P('dp', None, 'chan'), may hold values from -6 to 6
Outputs:
- output: bfloat16 [192, 152, 800], P('dp', None, 'chan')
- grad_inputs: float32 [192, 152, 800], P('dp', None, 'chan')
- grad_kernel: float32 [7, 7, 800], P(None, None, 'chan')
- grad_conv_bias: float32 [800], P('chan')
- grad_gain: float32 [800], P('chan')
- grad_norm_bias: float32 [800], P('chan')
- grad_weight_in: float32 [800, 3200], P(None, 'chan')
- grad_bias_in: float32 [3200], P('chan')
- grad_weight_out: float32 [3200, 800], P('chan')
- grad_bias_out: float32 [800], P('chan')
All inputs are finite; a program needn't handle non-finite values. No bound on the sum of `ocean_mask` on one device may be relied on, other than what follows from the above.
Results may differ from a plain program's by a relative error of at most 0.0057.
Values may be sent and summed in bfloat16 or wider, within the bound.
No kernel may reach another device: no remote copies, remote signals or barrier semaphores. Data moves between devices by JAX's collectives and lax.ppermute only.
A program may use at most 192 MiB of HBM per device.

v0:
```python
import jax
import jax.numpy as jnp
from jax import lax
from jax.experimental import pallas as pl
from jax.experimental.pallas import tpu as pltpu
from jax.sharding import PartitionSpec as P

CH = 800
GROUPS = 8
HISTORY = 2
SPAN = 2
EPSILON = 1e-05
GROUP_SIZE = CH // GROUPS
PARTS = 4
HALVES = 2
STEPS = 4
CHUNKS = 3
TILE = 256
COST = pl.CostEstimate(flops=4096, bytes_accessed=4096, transcendentals=0)
LANES = 256
F32 = jnp.float32
BF16 = jnp.bfloat16
VMEM = pl.BlockSpec(memory_space=pltpu.VMEM)
SMEM = pl.BlockSpec(memory_space=pltpu.SMEM)


def flipped(block, axis, bit):
    count = lax.axis_size(axis)
    return lax.ppermute(block, axis, [(place, place ^ bit) for place in range(count)])


def routed(block, allowed, partner):
    count, depth = lax.axis_size("dp"), lax.axis_size("chan")
    route = []
    for place in range(count):
        for level in range(depth):
            if allowed(place, level):
                to_place, to_level = partner(place, level)
                route.append((place * depth + level, to_place * depth + to_level))
    return lax.ppermute(block, ("dp", "chan"), route)


def lane_spans(channels):
    return [(start, min(128, channels - start)) for start in range(0, channels, 128)]


def by_lane_tile(rows):
    count, channels = rows.shape
    tiles = len(lane_spans(channels))
    padded = jnp.pad(rows, ((0, 0), (0, tiles * 128 - channels)))
    return padded.reshape(count, tiles, 128).transpose(1, 0, 2)


def summed(terms):
    while len(terms) > 1:
        terms = [terms[i] + terms[i + 1] for i in range(0, len(terms) - 1, 2)] + terms[len(terms) & ~1 :]
    return terms[0]


def fill_frame(pad_ref, rim_ref, within, first, height, across, spans, load):
    rows = pad_ref.shape[1]

    def store(at, row):
        for tile, (start, width) in enumerate(spans):
            pad_ref[tile, at, 8 : 8 + across, 0:width] = row[:, start : start + width]

    inner = [at for at in range(rows) if 0 <= first - 3 + at < height]

    def fill(at, carry):
        store(at, load(at + first - 3))
        return carry

    lax.fori_loop(inner[0], inner[-1] + 1, fill, 0)
    for at in range(rows):
        source = first - 3 + at
        if source < 0:
            store(at, rim_ref[source + 3].astype(F32) * (within == 1).astype(F32))
        elif source >= height:
            store(at, rim_ref[source - height].astype(F32) * (within == 0).astype(F32))

    def sides(at, carry):
        for tile in range(len(spans)):
            pad_ref[tile, at, 0:8, :] = jnp.zeros((8, 128), F32)
            pad_ref[tile, at, 8 + across : 16 + across, :] = jnp.zeros((8, 128), F32)
        return carry

    lax.fori_loop(0, rows, sides, 0)


def depthwise_kernel(half, within_ref, x_ref, rim_ref, wet_ref, keep_ref, taps_ref, bias_ref, *refs):
    before_ref = refs[0] if half else None
    out_ref, stat_ref, pad_ref, sum_ref = refs[half:]
    height, across, channels = x_ref.shape
    rows = height // HALVES
    row_block = rows
    spans = lane_spans(channels)
    keep = keep_ref[...]
    load = lambda row: x_ref[row].astype(F32) * wet_ref[row] * keep
    fill_frame(pad_ref, rim_ref, within_ref[0], half * rows, height, across, spans, load)
    sum_ref[...] = jnp.zeros_like(sum_ref)
    strips = across // 8
    for tile, (start, width) in enumerate(spans):

        def block(index, carry, tile=tile, start=start, width=width):
            row = index // strips * row_block
            col = pl.multiple_of(index % strips * 8, 8)
            acc = [jnp.broadcast_to(bias_ref[tile : tile + 1, :], (8, 128))] * row_block
            for b in range(7):
                lines = [pad_ref[tile, row + i, pl.ds(col + 5 + b, 8), :] for i in range(row_block + 6)]
                tap = [jnp.broadcast_to(taps_ref[tile, a * 7 + b : a * 7 + b + 1, :], (8, 128)) for a in range(7)]
                for i in range(row_block):
                    acc[i] = acc[i] + summed([lines[i + a] * tap[a] for a in range(7)])
            total = acc[0]
            for i in range(row_block):
                out_ref[row + i, pl.ds(col, 8), start : start + width] = acc[i][:, :width]
                if i:
                    total = total + acc[i]
            sum_ref[tile] += total
            return carry

        lax.fori_loop(0, rows // row_block * strips, block, 0)
    cells = rows * across
    for tile, (start, width) in enumerate(spans):
        mean = jnp.sum(sum_ref[tile], axis=0, keepdims=True)[:, :width] / cells

        def deviations(row, total, start=start, width=width, mean=mean):
            offset = out_ref[row, :, start : start + width] - mean
            return total + jnp.sum((offset * offset).reshape(strips, 8, width), axis=0)

        squares = lax.fori_loop(0, rows, deviations, jnp.zeros((8, width), F32))
        squares = jnp.sum(squares, axis=0, keepdims=True)
        if half:
            other = before_ref[0:1, start : start + width]
            squares = squares + before_ref[1:2, start : start + width] + (mean - other) * (mean - other) * (cells / 2)
            mean = 0.5 * (mean + other)
        stat_ref[0:1, start : start + width] = mean
        stat_ref[1:2, start : start + width] = squares


def depthwise(half, within, x, rim, wet, keep, taps, bias, *before):
    height, across, channels = x.shape
    rows = height // HALVES
    tiles = len(lane_spans(channels))

    def kernel(*refs):
        depthwise_kernel(half, *refs)

    return pl.pallas_call(
        kernel,
        out_shape=(
            jax.ShapeDtypeStruct((rows, across, channels), F32),
            jax.ShapeDtypeStruct((2, channels), F32),
        ),
        in_specs=[SMEM] + [VMEM] * (6 + half),
        out_specs=(VMEM, VMEM),
        scratch_shapes=[
            pltpu.VMEM((tiles, rows + 6, across + 16, 128), F32),
            pltpu.VMEM((tiles, 8, 128), F32),
        ],
        compiler_params=pltpu.CompilerParams(vmem_limit_bytes=16 << 20),
        cost_estimate=COST,
        name="depthwise" + "ab"[half],
    )(within, x, rim, wet, keep, taps, bias, *before)


def depthwise_back_kernel(step, within_ref, grad_ref, rim_ref, x_ref, cot_ref, wet_ref, keep_ref, taps_ref, *refs):
    out_ref, tap_grad_ref, pad_ref, acc_ref = refs[2 * (step > 0) :]
    height, across, channels = grad_ref.shape
    rows = height // STEPS
    row_block = rows
    spans = lane_spans(channels)
    fill_frame(pad_ref, rim_ref, within_ref[0], step * rows, height, across, spans, lambda row: grad_ref[row])
    acc_ref[...] = jnp.zeros_like(acc_ref)
    strips = across // 8
    for tile, (start, width) in enumerate(spans):

        def block(index, carry, tile=tile, start=start, width=width):
            row = index // strips * row_block
            col = pl.multiple_of(index % strips * 8, 8)
            here = (pl.ds(col, 8), slice(start, start + width))
            keep = jnp.broadcast_to(keep_ref[0:1, start : start + width], (8, width))
            mask = [wet_ref[row + i, pl.ds(col, 8), :] * keep for i in range(row_block)]
            masked = [x_ref[row + i, here[0], here[1]].astype(F32) * mask[i] for i in range(row_block)]
            acc = [cot_ref[row + i, here[0], here[1]].astype(F32) for i in range(row_block)]
            for b in range(7):
                lines = [pad_ref[tile, row + i, pl.ds(col + 5 + b, 8), 0:width] for i in range(row_block + 6)]
                tap = [
                    jnp.broadcast_to(taps_ref[tile, t : t + 1, 0:width], (8, width))
                    for t in range(48 - b, -1, -7)
                ]
                for i in range(row_block):
                    acc[i] = acc[i] + summed([lines[i + a] * tap[a] for a in range(7)])
                for a in range(7):
                    acc_ref[tile, (6 - a) * 7 + (6 - b), :, 0:width] += summed(
                        [lines[i + a] * masked[i] for i in range(row_block)]
                    )
            for i in range(row_block):
                out_ref[row + i, here[0], here[1]] = acc[i] * mask[i]
            return carry

        lax.fori_loop(0, rows // row_block * strips, block, 0)
    for tile, (start, width) in enumerate(spans):
        taps = jnp.sum(acc_ref[tile], axis=1)[:, 0:width]
        if step:
            taps = taps + refs[1][:, start : start + width]
        tap_grad_ref[:, start : start + width] = taps


def depthwise_back(step, within, grad, rim, x, cot, wet, keep, taps, *before):
    height, across, channels = x.shape
    rows = height // STEPS
    tiles = len(lane_spans(channels))
    part = lambda minor: pl.BlockSpec((rows, across, minor), lambda i: (step, 0, 0))

    def kernel(*refs):
        depthwise_back_kernel(step, *refs)

    return pl.pallas_call(
        kernel,
        grid=(1,),
        out_shape=(jax.ShapeDtypeStruct(x.shape, F32), jax.ShapeDtypeStruct((49, channels), F32)),
        in_specs=[SMEM, VMEM, VMEM, part(channels), part(channels), part(1), VMEM, VMEM]
        + [pl.BlockSpec(memory_space=pl.ANY), VMEM] * (step > 0),
        out_specs=(part(channels), pl.BlockSpec((49, channels), lambda i: (0, 0))),
        scratch_shapes=[
            pltpu.VMEM((tiles, rows + 6, across + 16, 128), F32),
            pltpu.VMEM((tiles, 49, 8, 128), F32),
        ],
        input_output_aliases={8: 0} if step else {},
        compiler_params=pltpu.CompilerParams(vmem_limit_bytes=20 << 20),
        cost_estimate=COST,
        name="depthwise_back_" + "abcd"[step],
    )(within, grad, rim, x, cot, wet, keep, taps, *before)


WIDE, MID, THIN = 128, 64, 8


def packed_rows(cells):
    return cells + cells // 2 + thin_run(cells)


def thin_run(cells):
    return -(-cells // (16 * 8)) * 8


def pieces_of(cells, channels):
    assert channels == WIDE + MID + THIN
    span = lambda first, size: slice(first, first + size)
    half, run = cells // 2, thin_run(cells)
    yield (span(0, cells), span(0, WIDE)), (span(0, cells), span(0, WIDE))
    for side in range(2):
        yield (span(cells, half), span(side * MID, MID)), (span(side * half, half), span(WIDE, MID))
    for group in range(-(-cells // run)):
        size = min(run, cells - group * run)
        yield (
            (span(cells + half, size), span(group * THIN, THIN)),
            (span(group * run, size), span(WIDE + MID, THIN)),
        )


def moved(rows, base):
    return slice(rows.start + base, rows.stop + base)


def pack(packed_ref, index, plain_ref, channels=WIDE + MID + THIN):
    cells = plain_ref.shape[0]
    base = index * packed_rows(cells)
    for (rows, lanes), (cell, channel) in pieces_of(cells, channels):
        packed_ref[moved(rows, base), lanes] = plain_ref[cell, channel].astype(BF16)


def unpack(packed_ref, index, plain_ref, channels=WIDE + MID + THIN):
    cells = plain_ref.shape[0]
    base = index * packed_rows(cells)
    for (rows, lanes), (cell, channel) in pieces_of(cells, channels):
        plain_ref[cell, channel] = packed_ref[moved(rows, base), lanes]


def group_total(row):
    channels = row.shape[1]
    group = lax.broadcasted_iota(jnp.int32, (1, channels), 1) // GROUP_SIZE
    total = jnp.zeros((1, channels), F32)
    for index in range(channels // GROUP_SIZE):
        member = group == index
        total = jnp.where(member, jnp.sum(jnp.where(member, row, 0.0), axis=1, keepdims=True), total)
    return total


def folded(value):
    rows, channels = value.shape
    return jnp.sum(value.reshape(rows // 8, 8, channels), axis=0)


def call(kernel, name, out_shape, specs, scratch=(), limit=12):
    many = isinstance(out_shape, tuple)
    return pl.pallas_call(
        kernel,
        out_shape=out_shape,
        in_specs=specs,
        out_specs=(VMEM,) * len(out_shape) if many else VMEM,
        scratch_shapes=scratch,
        compiler_params=pltpu.CompilerParams(vmem_limit_bytes=limit << 20),
        cost_estimate=COST,
        name=name,
    )


def packed_shape(cells, channels):
    return jax.ShapeDtypeStruct((PARTS * packed_rows(cells // PARTS), WIDE), BF16)


def plain_scratch(cells, channels):
    return pltpu.VMEM((PARTS, cells // PARTS, channels), BF16)


def cut_kernel(cot_ref, wet_ref, packed_ref, bias_ref, plain_ref):
    height, across, channels = cot_ref.shape
    total = jnp.zeros((8, channels), F32)
    for index in range(PARTS):
        rows = height // PARTS

        def one(row, total, index=index, rows=rows):
            grad = (cot_ref[index * rows + row].astype(F32) * wet_ref[index * rows + row]).astype(BF16)
            plain_ref[index, pl.ds(pl.multiple_of(row * across, 8), across), :] = grad
            return total + folded(grad.astype(F32))

        total = lax.fori_loop(0, rows, one, total)
        pack(packed_ref, index, plain_ref.at[index])
    bias_ref[...] = jnp.sum(total, axis=0, keepdims=True)


def cut(cot, wet):
    height, across, channels = cot.shape
    out_shape = (packed_shape(height * across, channels), jax.ShapeDtypeStruct((1, channels), F32))
    scratch = [plain_scratch(height * across, channels)]
    return call(cut_kernel, "cut", out_shape, [VMEM, VMEM], scratch)(cot, wet)


def norm_kernel(*refs):
    conv = refs[:HALVES]
    stat_ref, other_ref, gain_ref, bias_ref, packed_ref, fit_ref, plain_ref = refs[HALVES:]
    rows, across, channels = conv[0].shape
    cells = HALVES * rows * across
    stat, other = stat_ref[...], other_ref[...]
    members = SPAN * GROUP_SIZE
    centre = group_total(stat[0:1] + other[0:1]) / members
    away, other_away = stat[0:1] - centre, other[0:1] - centre
    squares = stat[1:2] + other[1:2] + cells * (away * away + other_away * other_away)
    inverse = lax.rsqrt(group_total(squares) / (members * cells) + EPSILON)
    fit_ref[0:1] = centre
    fit_ref[1:2] = inverse
    gain, bias = gain_ref[...], bias_ref[...]
    for index in range(PARTS):
        half, first = divmod(index * HALVES * rows // PARTS, rows)

        def one(row, carry, index=index, half=half, first=first):
            standard = (conv[half][first + row] - centre) * inverse
            at = pl.multiple_of(row * across, 8)
            plain_ref[index, pl.ds(at, across), :] = (standard * gain + bias).astype(BF16)
            return carry

        lax.fori_loop(0, HALVES * rows // PARTS, one, 0)
        pack(packed_ref, index, plain_ref.at[index])


def norm(conv, stat, other, gain, bias):
    rows, across, channels = conv[0].shape
    cells = HALVES * rows * across
    out_shape = (packed_shape(cells, channels), jax.ShapeDtypeStruct((2, channels), F32))
    size = cells * channels
    scratch = [plain_scratch(cells, channels)]
    return call(norm_kernel, "norm", out_shape, [VMEM] * (4 + HALVES), scratch)(
        *conv, stat, other, gain, bias
    )


def moments_kernel(*refs):
    conv = refs[:HALVES]
    fit_ref, packed_ref, sums_ref, back_ref = refs[HALVES:]
    rows, across, channels = conv[0].shape
    centre, inverse = fit_ref[0:1], fit_ref[1:2]
    sums = (jnp.zeros((8, channels), F32), jnp.zeros((8, channels), F32))
    for index in range(PARTS):
        half, first = divmod(index * HALVES * rows // PARTS, rows)
        unpack(packed_ref, index, back_ref.at[index])

        def one(row, sums, index=index, half=half, first=first):
            standard = (conv[half][first + row] - centre) * inverse
            grad = back_ref[index, pl.ds(pl.multiple_of(row * across, 8), across), :].astype(F32)
            return sums[0] + folded(grad), sums[1] + folded(grad * standard)

        sums = lax.fori_loop(0, HALVES * rows // PARTS, one, sums)
    sums_ref[0:1] = jnp.sum(sums[0], axis=0, keepdims=True)
    sums_ref[1:2] = jnp.sum(sums[1], axis=0, keepdims=True)


def moments(conv, fit, packed):
    rows, across, channels = conv[0].shape
    cells = HALVES * rows * across
    out_shape = (
        jax.ShapeDtypeStruct((2, channels), F32),
        jax.ShapeDtypeStruct((PARTS, cells // PARTS, channels), BF16),
    )
    size = cells * channels
    return call(moments_kernel, "moments", out_shape, [VMEM] * (2 + HALVES))(*conv, fit, packed)


def norm_back_kernel(within_ref, *refs):
    conv = refs[:HALVES]
    fit_ref, back_ref, sums_ref, other_ref, gain_ref, grad_ref, rim_ref, bias_ref = refs[HALVES:]
    rows, across, channels = conv[0].shape
    members = SPAN * GROUP_SIZE * HALVES * rows * across
    centre, inverse = fit_ref[0:1], fit_ref[1:2]
    gain = gain_ref[...]
    sums = sums_ref[...] + other_ref[...]
    mean_first = group_total(sums[0:1] * gain) / members
    mean_second = group_total(sums[1:2] * gain) / members
    total = jnp.zeros((8, channels), F32)
    for index in range(PARTS):
        half, first = divmod(index * HALVES * rows // PARTS, rows)

        def one(row, total, index=index, half=half, first=first):
            standard = (conv[half][first + row] - centre) * inverse
            grad = back_ref[index, pl.ds(pl.multiple_of(row * across, 8), across), :].astype(F32)
            grad = inverse * (grad * gain - mean_first - standard * mean_second)
            grad_ref[half * rows + first + row] = grad
            return total + folded(grad)

        total = lax.fori_loop(0, HALVES * rows // PARTS, one, total)
    bias_ref[...] = jnp.sum(total, axis=0, keepdims=True)
    edge = jnp.where(within_ref[0] == 0, HALVES * rows - 3, 0)
    for index in range(3):
        rim_ref[index] = grad_ref[edge + index].astype(BF16)


def norm_back(within, conv, fit, back, sums, other, gain):
    rows, across, channels = conv[0].shape
    out_shape = (
        jax.ShapeDtypeStruct((HALVES * rows, across, channels), F32),
        jax.ShapeDtypeStruct((3, across, channels), BF16),
        jax.ShapeDtypeStruct((1, channels), F32),
    )
    specs = [SMEM] + [VMEM] * (5 + HALVES)
    return call(norm_back_kernel, "norm_back", out_shape, specs)(
        within, *conv, fit, back, sums, other, gain
    )


def finish_kernel(x_ref, wet_ref, keep_ref, bias_ref, packed_ref, out_ref, plain_ref):
    height, across, channels = x_ref.shape
    keep, bias = keep_ref[...], bias_ref[...]
    rows = height // PARTS
    for index in range(PARTS):
        unpack(packed_ref, index, plain_ref.at[index])

        def one(row, carry, index=index):
            branch = plain_ref[index, pl.ds(pl.multiple_of(row * across, 8), across), :].astype(F32) + bias
            masked = x_ref[index * rows + row].astype(F32) * keep
            out_ref[index * rows + row] = (wet_ref[index * rows + row] * (masked + branch)).astype(BF16)
            return carry

        lax.fori_loop(0, rows, one, 0)


def finish(x, wet, keep, bias, packed):
    height, across, channels = x.shape
    out_shape = jax.ShapeDtypeStruct(x.shape, BF16)
    scratch = [plain_scratch(height * across, channels)]
    return call(finish_kernel, "finish", out_shape, [VMEM] * 5, scratch)(x, wet, keep, bias, packed)


def join_kernel(own_ref, far_ref, sum_ref):
    sum_ref[...] = (own_ref[...].astype(F32) + far_ref[...].astype(F32)).astype(BF16)


def join(own, far):
    out_shape = jax.ShapeDtypeStruct(own.shape, BF16)
    return call(join_kernel, "join", out_shape, [VMEM] * 2)(own, far)


TURNED = (((1,), (1,)), ((), ()))


def piece_shape(part, units):
    full, tail = divmod(units, WIDE)
    rows = 2 * part + 8
    runs = WIDE // tail
    run = -(-rows // (8 * runs)) * 8
    return full, tail, rows, run


def piece_moves(part, units):
    full, tail, rows, run = piece_shape(part, units)
    for kind, first, count in ((0, 0, part), (1, part, part), (2, 2 * part, 8)):
        for tile in range(full):
            lanes = slice(tile * WIDE, (tile + 1) * WIDE)
            at = tile * rows + first
            yield kind, slice(0, count), lanes, slice(at, at + count), slice(0, WIDE)
        row = first
        while row < first + count:
            group = row // run
            stop = min(first + count, (group + 1) * run)
            at = full * rows + row - group * run
            yield (
                kind,
                slice(row - first, stop - first),
                slice(full * WIDE, units),
                slice(at, at + stop - row),
                slice(group * tail, (group + 1) * tail),
            )
            row = stop


def prepare_kernel(in_ref, out_ref, bias_ref, packed_ref, digits_ref):
    part, units = in_ref.shape
    rest = bias_ref[...]
    digits = []
    for _ in range(3):
        digits.append(rest.astype(BF16).astype(F32))
        rest = rest - digits[-1]
    digits_ref[...] = jnp.concatenate(digits + [jnp.zeros((5, units), F32)]).astype(BF16)
    sources = (in_ref, out_ref, digits_ref)
    for kind, rows, lanes, packed_rows_, packed_lanes in piece_moves(part, units):
        packed_ref[packed_rows_, packed_lanes] = sources[kind][rows, lanes]


def prepare(in_rows, out_rows, bias):
    part, units = in_rows.shape
    full, _, rows, run = piece_shape(part, units)
    out_shape = jax.ShapeDtypeStruct((full * rows + run, WIDE), BF16)
    return call(prepare_kernel, "prepare", out_shape, [VMEM] * 3, [pltpu.VMEM((8, units), BF16)])(
        in_rows, out_rows, bias
    )


def spread_weights(pieces, weight_ref, bias_ref, digits_ref, quarter, units, part):
    slot_lanes = weight_ref.shape[2] // 2
    for slot in range(2):
        first = slot * slot_lanes
        for j in range(PARTS):
            piece = pieces[slot * PARTS + j]
            base = pl.multiple_of((quarter ^ j) * LANES, LANES)
            for kind, rows, lanes, packed_rows_, packed_lanes in piece_moves(part, units):
                value = piece[packed_rows_, packed_lanes]
                if kind < 2:
                    at = pl.ds(base + rows.start, rows.stop - rows.start)
                    weight_ref[kind, at, first + lanes.start : first + lanes.stop] = value
                elif j == 0:
                    digits_ref[:, lanes] = value
            for kind in range(2):
                weight_ref[kind, pl.ds(base, part), first + units : first + slot_lanes] = jnp.zeros(
                    (part, slot_lanes - units), BF16
                )
        digits = digits_ref[...].astype(F32)
        bias_ref[0:1, first : first + units] = digits[0:1] + digits[1:2] + digits[2:3]
        bias_ref[0:1, first + units : first + slot_lanes] = jnp.zeros((1, slot_lanes - units), F32)
    for kind in range(2):
        for c in range(PARTS):
            weight_ref[kind, c * LANES + part : (c + 1) * LANES, :] = jnp.zeros((LANES - part, 2 * slot_lanes), BF16)


def spread_cells(packed_ref, plain_ref, turned_ref, channels, filler):
    cells = plain_ref.shape[0]
    for c in range(PARTS):
        view = plain_ref.at[:, c * LANES : (c + 1) * LANES]
        unpack(packed_ref, c, view)
        view[:, channels:LANES] = jnp.zeros((cells, LANES - channels), BF16)
        turned_ref[c, 0:channels, :] = view[:, 0:channels].T
        turned_ref[c, channels : channels + 8, :] = filler


def lane_tiles(lanes):
    return [slice(first, first + TILE) for first in range(0, lanes, TILE)]


def rows_here(cells):
    size = cells // CHUNKS
    step = pl.program_id(0)
    return step // CHUNKS, pl.ds(pl.multiple_of(step % CHUNKS * size, 16), size)


def forward_kernel(units, quarter_ref, *refs):
    packed = refs[:2]
    pieces = refs[2 : 2 + 2 * PARTS]
    own_ref, far_ref, active_ref, slope_ref, turned_out_ref, weight_out_ref = refs[2 + 2 * PARTS : 8 + 2 * PARTS]
    acts_ref, turned_ref, weight_ref, bias_ref, digits_ref, branch_ref, sems = refs[8 + 2 * PARTS :]
    cells = acts_ref.shape[1]
    channels = turned_ref.shape[2] - 8
    outward = [
        pltpu.make_async_copy(weight_ref, weight_out_ref, sems.at[0]),
        pltpu.make_async_copy(turned_ref, turned_out_ref, sems.at[1]),
    ]

    @pl.when(pl.program_id(0) == 0)
    def _():
        spread_weights(pieces, weight_ref, bias_ref, digits_ref, quarter_ref[0], units, channels)
        outward[0].start()
        ones = (lax.broadcasted_iota(jnp.int32, (8, cells), 0) == 0).astype(BF16)
        for side in range(2):
            spread_cells(packed[side], acts_ref.at[side], turned_ref.at[side], channels, ones)
        outward[1].start()

    side, rows = rows_here(cells)
    for tile in lane_tiles(weight_ref.shape[2]):
        value = jnp.dot(acts_ref[side, rows, :], weight_ref[0, :, tile], preferred_element_type=F32)
        value = value + bias_ref[0:1, tile]
        cumulative = 0.5 * (1.0 + lax.erf(value * 0.7071067811865476))
        density = jnp.exp(-0.5 * value * value) * 0.3989422804014327
        active_ref[0, :, tile] = (value * cumulative).astype(BF16)
        slope_ref[0, :, tile] = cumulative + value * density
    branch = lax.dot_general(active_ref[0], weight_ref[1], TURNED, preferred_element_type=F32)
    branch_ref[side, rows, :] = branch.astype(BF16)

    @pl.when(pl.program_id(0) == pl.num_programs(0) - 1)
    def _():
        for side, out_ref in enumerate((own_ref, far_ref)):
            for c in range(PARTS):
                pack(out_ref, c, branch_ref.at[side, :, c * LANES : (c + 1) * LANES])
        for copy in outward:
            copy.wait()


def whole(*shape):
    return pl.BlockSpec(shape, lambda t: (0,) * len(shape), pipeline_mode=pl.Buffered(1))


ANYWHERE = pl.BlockSpec(memory_space=pl.ANY)


def forward(quarter, acts, pieces, units, cells, channels):
    rows = acts[0].shape[0]
    slot_lanes = -(-units // 128) * 128
    lanes = 2 * slot_lanes
    chunk = pl.BlockSpec((1, cells // CHUNKS, lanes), lambda t: (t // CHUNKS, t % CHUNKS, 0))

    def kernel(*refs):
        forward_kernel(units, *refs)

    return pl.pallas_call(
        kernel,
        grid=(2 * CHUNKS,),
        out_shape=(
            jax.ShapeDtypeStruct((rows, WIDE), BF16),
            jax.ShapeDtypeStruct((rows, WIDE), BF16),
            jax.ShapeDtypeStruct((2, cells, lanes), BF16),
            jax.ShapeDtypeStruct((2, cells, lanes), F32),
            jax.ShapeDtypeStruct((2, PARTS, channels + 8, cells), BF16),
            jax.ShapeDtypeStruct((2, PARTS * LANES, lanes), BF16),
        ),
        in_specs=[SMEM] + [whole(rows, WIDE)] * 2 + [whole(*pieces[0].shape)] * (2 * PARTS),
        out_specs=(whole(rows, WIDE),) * 2 + (chunk, chunk, ANYWHERE, ANYWHERE),
        scratch_shapes=[
            pltpu.VMEM((2, cells, PARTS * LANES), BF16),
            pltpu.VMEM((2, PARTS, channels + 8, cells), BF16),
            pltpu.VMEM((2, PARTS * LANES, lanes), BF16),
            pltpu.VMEM((1, lanes), F32),
            pltpu.VMEM((8, units), BF16),
            pltpu.VMEM((2, cells, PARTS * LANES), BF16),
            pltpu.SemaphoreType.DMA((2,)),
        ],
        compiler_params=pltpu.CompilerParams(vmem_limit_bytes=60 << 20, dimension_semantics=("arbitrary",)),
        cost_estimate=COST,
        name="forward",
    )(quarter, *acts, *pieces)


def backward_kernel(*refs):
    packed = refs[:2]
    weight_in_ref, slope_ref, own_ref, far_ref, grad_hidden_ref, turned_out_ref = refs[2:8]
    grads_ref, turned_ref, weight_ref, sems = refs[8:]
    step = pl.program_id(0)
    cells = grads_ref.shape[1]
    lanes = weight_ref.shape[2]
    channels = turned_ref.shape[2] - 8
    inward = pltpu.make_async_copy(weight_in_ref, weight_ref, sems.at[0])
    outward = pltpu.make_async_copy(turned_ref, turned_out_ref, sems.at[1])

    @pl.when(step == 0)
    def _():
        inward.start()
        zeros = jnp.zeros((8, cells), BF16)
        for side in range(2):
            spread_cells(packed[side], grads_ref.at[side], turned_ref.at[side], channels, zeros)
        outward.start()
        inward.wait()

    side, rows = rows_here(cells)
    for tile in lane_tiles(lanes):
        grad = jnp.dot(grads_ref[side, rows, :], weight_ref[1, :, tile], preferred_element_type=F32)
        grad_hidden_ref[0, :, tile] = (grad * slope_ref[0, :, tile]).astype(BF16)
    back = lax.dot_general(grad_hidden_ref[0], weight_ref[0], TURNED, preferred_element_type=F32)
    grads_ref[side, rows, :] = back.astype(BF16)

    @pl.when(step == pl.num_programs(0) - 1)
    def _():
        for side, out_ref in enumerate((own_ref, far_ref)):
            for c in range(PARTS):
                pack(out_ref, c, grads_ref.at[side, :, c * LANES : (c + 1) * LANES])
        outward.wait()


def backward(grads, weights, slope, channels):
    rows = grads[0].shape[0]
    lanes = weights.shape[2]
    cells = slope.shape[1]
    chunk = pl.BlockSpec((1, cells // CHUNKS, lanes), lambda t: (t // CHUNKS, t % CHUNKS, 0))
    return pl.pallas_call(
        backward_kernel,
        grid=(2 * CHUNKS,),
        out_shape=(jax.ShapeDtypeStruct((rows, WIDE), BF16),) * 2
        + (
            jax.ShapeDtypeStruct((2, cells, lanes), BF16),
            jax.ShapeDtypeStruct((2, PARTS, channels + 8, cells), BF16),
        ),
        in_specs=[whole(rows, WIDE)] * 2 + [ANYWHERE, chunk],
        out_specs=(whole(rows, WIDE),) * 2 + (chunk, ANYWHERE),
        scratch_shapes=[
            pltpu.VMEM((2, cells, PARTS * LANES), BF16),
            pltpu.VMEM((2, PARTS, channels + 8, cells), BF16),
            pltpu.VMEM((2, PARTS * LANES, lanes), BF16),
            pltpu.SemaphoreType.DMA((2,)),
        ],
        compiler_params=pltpu.CompilerParams(vmem_limit_bytes=60 << 20, dimension_semantics=("arbitrary",)),
        cost_estimate=COST,
        name="backward",
    )(*grads, weights, slope)


def weight_grads_kernel(quarter_ref, left_ref, right_ref, *refs):
    outs, sum_ref = refs[:PARTS], refs[PARTS]
    _, parts, rows, cells = left_ref.shape
    grad = jnp.dot(left_ref[0].reshape(parts * rows, cells), right_ref[0], preferred_element_type=F32)
    grad = grad + jnp.dot(left_ref[1].reshape(parts * rows, cells), right_ref[1], preferred_element_type=F32)
    sum_ref[...] = grad.reshape(parts, rows, grad.shape[1])
    for j in range(PARTS):
        outs[j][...] = sum_ref[quarter_ref[0] ^ j].astype(outs[j].dtype)


def weight_grads(quarter, left, right, name):
    _, parts, rows, cells = left.shape
    lanes = right.shape[2]
    return pl.pallas_call(
        weight_grads_kernel,
        grid=(lanes // TILE,),
        out_shape=(jax.ShapeDtypeStruct((rows, lanes), F32),) + (jax.ShapeDtypeStruct((rows, lanes), BF16),) * 3,
        in_specs=[SMEM, whole(*left.shape), pl.BlockSpec((2, cells, TILE), lambda t: (0, 0, t))],
        out_specs=(pl.BlockSpec((rows, TILE), lambda t: (0, t)),) * PARTS,
        scratch_shapes=[pltpu.VMEM((parts, rows, TILE), F32)],
        compiler_params=pltpu.CompilerParams(vmem_limit_bytes=60 << 20, dimension_semantics=("arbitrary",)),
        cost_estimate=COST,
        name=name,
    )(quarter, left, right)


def slots_kernel(own_ref, *refs):
    came, (keep_ref, send_ref) = refs[:3], refs[3:]
    lanes = keep_ref.shape[1]
    for first in (0, lanes):
        here = slice(first, first + lanes)
        total = own_ref[:, here]
        for ref in came:
            total = total + ref[:, here].astype(F32)
        if first:
            send_ref[...] = total.astype(BF16)
        else:
            keep_ref[...] = total


def slots(own, *came):
    rows, lanes = own.shape
    out_shape = (jax.ShapeDtypeStruct((rows, lanes // 2), F32), jax.ShapeDtypeStruct((rows, lanes // 2), BF16))
    return call(slots_kernel, "slots", out_shape, [VMEM] * 4)(own, *came)


def add_kernel(keep_ref, came_ref, own_ref, send_ref):
    total = keep_ref[...] + came_ref[...].astype(F32)
    own_ref[...] = total
    send_ref[...] = total.astype(BF16)


def add(keep, came):
    out_shape = (jax.ShapeDtypeStruct(keep.shape, F32), jax.ShapeDtypeStruct(keep.shape, BF16))
    return call(add_kernel, "add", out_shape, [VMEM] * 2)(keep, came)


def gather_kernel(place_ref, *refs):
    near, far = refs[:PARTS], refs[PARTS : 2 * PARTS]
    in_ref, out_ref, bias_ref, held_ref = refs[2 * PARTS :]
    core, quarter = place_ref[0], place_ref[1]
    for j in range(PARTS):
        held_ref[core, quarter ^ j] = near[j][...]
        held_ref[1 - core, quarter ^ j] = far[j][...]
    units = in_ref.shape[1]
    channels = in_ref.shape[0] // PARTS
    for c in range(PARTS):
        in_ref[c * channels : (c + 1) * channels, :] = held_ref[0, c, 0:channels, 0:units].astype(F32)
        out_ref[:, c * channels : (c + 1) * channels] = held_ref[1, c, 0:channels, 0:units].astype(F32).T
    bias_ref[...] = held_ref[0, 0, channels : channels + 8, 0:units].astype(F32)[0:1]


def gather(place, near, far, channels, units):
    rows, lanes = near[0].shape
    return pl.pallas_call(
        gather_kernel,
        out_shape=(
            jax.ShapeDtypeStruct((PARTS * channels, units), F32),
            jax.ShapeDtypeStruct((units, PARTS * channels), F32),
            jax.ShapeDtypeStruct((1, units), F32),
        ),
        in_specs=[SMEM] + [VMEM] * (2 * PARTS),
        out_specs=(VMEM,) * 3,
        scratch_shapes=[pltpu.VMEM((2, PARTS, rows, lanes), BF16)],
        compiler_params=pltpu.CompilerParams(vmem_limit_bytes=16 << 20),
        cost_estimate=COST,
        name="gather",
    )(place, *near, *far)


def after(value, *earlier):
    return lax.optimization_barrier((value, earlier))[0]


def body(
    inputs,
    ocean_mask,
    counts,
    kernel,
    conv_bias,
    norm_gain,
    norm_bias,
    weight_in,
    bias_in,
    weight_out,
    bias_out,
    cotangent,
):
    height, across, channels = inputs.shape
    units = weight_in.shape[1]
    place = lax.axis_index("dp")
    level = lax.axis_index("chan")
    core = place % SPAN
    quarter = place // SPAN % PARTS
    mine = level // 2 == core
    scalar = lambda value: value.astype(jnp.int32).reshape(1)
    row = lambda vector: vector.reshape(1, channels)
    core_of = lambda at: at % SPAN
    owner = lambda at, lev: lev // 2 == core_of(at)
    stranger = lambda at, lev: lev // 2 != core_of(at)
    up_two = lambda at, lev: (at, lev ^ 2)

    piece = prepare(
        lax.dynamic_slice_in_dim(weight_in, quarter * channels, channels, 0),
        lax.dynamic_slice_in_dim(weight_out, quarter * channels, channels, 1).T,
        bias_in.reshape(1, units),
    )
    far_piece = routed(piece, owner, up_two)

    sample = place // SPAN
    count_here = jnp.sum(jnp.where(jnp.arange(counts.shape[0]) == sample, counts, 0))
    channel = level * channels + jnp.arange(channels)
    keep = (channel // (CH // HISTORY) < count_here).astype(F32).reshape(1, channels)
    wet = ocean_mask.astype(F32)[:, :, None]
    edge = jnp.where(core == 0, height - 3, 0)
    outgoing = (
        lax.dynamic_slice_in_dim(inputs, edge, 3, 0).astype(F32) * lax.dynamic_slice_in_dim(wet, edge, 3, 0) * keep
    ).astype(BF16)
    rim = flipped(outgoing, "dp", 1)
    taps = by_lane_tile(kernel.reshape(49, channels))
    bias = by_lane_tile(row(conv_bias))[:, 0]
    upper, upper_stat = depthwise(0, scalar(core), inputs, rim, wet, keep, taps, bias)
    slot = jnp.where(mine, piece, after(far_piece, upper_stat))
    lower, stat = depthwise(1, scalar(core), inputs, rim, wet, keep, taps, bias, after(upper_stat, slot))
    conv = [upper, lower]
    other_slot = flipped(slot, "chan", 1)
    beside, below = flipped(slot, "dp", 2), flipped(slot, "dp", 4)
    stat = after(stat, (other_slot, beside, below))
    normed, fit = norm(conv, stat, flipped(stat, "dp", 1), row(norm_gain), row(norm_bias))
    other_below = flipped(other_slot, "dp", 4)
    grad_branch, grad_bias_out = cut(after(cotangent, normed), wet)
    pieces = [
        slot,
        beside,
        below,
        flipped(after(beside, other_below), "dp", 4),
        other_slot,
        flipped(other_slot, "dp", 2),
        other_below,
        flipped(other_below, "dp", 2),
    ]

    exchanged = lambda cells: lax.all_to_all(cells, "chan", 0, 0, tiled=True)
    other_core = lambda cells: flipped(cells, "dp", 1)
    here = scalar(quarter)
    normed = after(exchanged(normed), (grad_branch, pieces))
    grad_branch = exchanged(after(grad_branch, normed))
    branch_own, branch_far, active, slope, turned, weights = forward(
        here, (normed, other_core(normed)), pieces, units, height // PARTS * across, channels
    )
    straight = lambda sends: [flipped(value, "dp", SPAN * (1 + at)) for at, value in enumerate(sends)]
    beyond = lambda value: routed(value, stranger, up_two)
    branch = join(branch_own, other_core(branch_far))
    grad_branch = after(grad_branch, branch)
    grad_cells = (grad_branch, other_core(grad_branch))
    branch = exchanged(branch)
    back_own, back_far, grad_hidden, turned_grad = backward(grad_cells, weights, slope, channels)
    out_own, *out_sends = weight_grads(here, after(turned_grad, back_own), active, "out_grads")
    back = join(after(back_own, (out_own, branch)), other_core(back_far))
    in_own, *in_sends = weight_grads(here, turned, after(grad_hidden, back), "in_grads")
    out_came = after(straight(out_sends), in_own)
    back = after(exchanged(back), out_came)

    sums, back = moments(after(conv, back), fit, back)
    grad_conv, outgoing_grad, grad_conv_bias = norm_back(
        scalar(core), conv, fit, back, sums, flipped(sums, "dp", 1), row(norm_gain)
    )
    grad_rim = flipped(outgoing_grad, "dp", 1)
    operands = (inputs, cotangent, wet, keep, taps)
    out_slot, out_send = slots(out_own, *after(out_came, grad_conv))
    partial = depthwise_back(0, scalar(core), grad_conv, after(grad_rim, out_send), *operands)
    out_slot, out_send = add(out_slot, after(flipped(out_send, "chan", 1), partial))
    partial = depthwise_back(1, scalar(core), grad_conv, after(grad_rim, out_send), *operands, *partial)
    in_slot, in_send = slots(in_own, *after(straight(in_sends), partial))
    partial = depthwise_back(2, scalar(core), grad_conv, after(grad_rim, in_send), *operands, *partial)
    in_slot, in_send = add(in_slot, after(flipped(in_send, "chan", 1), partial))
    _, out_sum = add(out_slot, after(beyond(out_send), in_send))
    grad_inputs, grad_taps = depthwise_back(
        3, scalar(core), grad_conv, after(grad_rim, (in_send, out_sum)), *operands, *partial
    )
    _, in_sum = add(in_slot, after(beyond(in_send), grad_taps))
    slot_sum = jnp.stack([in_sum, out_sum])
    bit = SPAN * PARTS
    while bit < lax.axis_size("dp"):
        slot_sum = (slot_sum.astype(F32) + flipped(slot_sum, "dp", bit).astype(F32)).astype(BF16)
        bit *= 2
    own_kind = jnp.where(core == 0, slot_sum[0], slot_sum[1])
    other_kind = jnp.where(core == 0, slot_sum[1], slot_sum[0])
    share = jnp.where(mine, own_kind, other_core(other_kind))
    small = jnp.concatenate(
        [grad_taps, grad_conv_bias, sums[1:2], sums[0:1], grad_bias_out, jnp.zeros((3, channels), F32)]
    )
    bit = 1
    while 2 * bit < lax.axis_size("dp"):
        small = small + flipped(small, "dp", bit)
        bit *= 2
    share = after(share, small)
    output = finish(inputs, wet, keep, row(bias_out), after(branch, share))
    shares = after([share] + [flipped(share, "dp", SPAN * j) for j in range(1, PARTS)], output)
    grad_weight_in, grad_weight_out, grad_bias_in = gather(
        jnp.stack([core, quarter]).astype(jnp.int32), shares, [other_core(value) for value in shares], channels, units
    )
    small = small + after(flipped(small, "dp", bit), grad_weight_in)
    return (
        output,
        grad_inputs,
        small[:49].reshape(7, 7, channels),
        small[49],
        small[50],
        small[51],
        grad_weight_in,
        grad_bias_in.reshape(units),
        grad_weight_out,
        small[52],
    )


def solution(mesh):
    in_specs = (
        P("dp", None, "chan"),
        P("dp", None),
        P(),
        P(None, None, "chan"),
        P("chan"),
        P("chan"),
        P("chan"),
        P(None, "chan"),
        P("chan"),
        P("chan", None),
        P("chan"),
        P("dp", None, "chan"),
    )
    out_specs = (
        P("dp", None, "chan"),
        P("dp", None, "chan"),
        P(None, None, "chan"),
        P("chan"),
        P("chan"),
        P("chan"),
        P(None, "chan"),
        P("chan"),
        P("chan", None),
        P("chan"),
    )
    return jax.shard_map(body, mesh=mesh, in_specs=in_specs, out_specs=out_specs, check_vma=False)
```

profile of v0, /device:TPU:0, one launch (start us, length us, event | category | flops | bytes accessed | tf_op | source)
XLA Modules:
  0.0 315.2 jit_solution(2692216756205968452)
XLA Ops:
  3.7 6.9 %collective-permute-start.1 = (bf16[2552,128]{1,0:T(8,128)(2,1)S(1)}, bf16[2552,128]{1,0:T(8,128)(2,1)}, u32[]{:S(2)}, u32[]{:S(2)}) collective-permute-start(bf16[2552,128]{1,0:T(8,128)(2,1)S(1)} %prepare.1), channel_id=1, source_target_pairs={{0,2},{1,3},{6,4},{7,5},{8,10},{9,11},{14,12},{15,13},{16,18},{17,... | collective-permute-start | bytes 1959944 | tf_op jit(solution)/shard_map/ppermute | solution.py:40
  16.1 10.0 %depthwisea.1 = (f32[12,152,200]{2,1,0:T(8,128)S(1)}, f32[2,200]{1,0:T(2,128)S(1)}) custom-call(s32[1]{0:T(128)} %bitcast.3.refs_0_.within_ref, bf16[24,152,200]{2,1,0:T(8,128)(2,1)S(1)} %copy-done.2, bf16[3,152,200]{2,1,0:T(8,128)(2,1)S(1)} %collective-permute-done.refs_2_, f32[24,152,1]{2,1,0:T(8,128)S(1)} %copy.35.refs_3_.wet_ref.refs_5_, ...), custom_call_target="tpu_custom_call" | custom-call | flops 4096 | bytes 4096 | tf_op jit(solution)/shard_map/depthwisea/pallas_call | solution.py:148
  31.0 10.0 %depthwiseb.1 = (f32[12,152,200]{2,1,0:T(8,128)S(1)}, f32[2,200]{1,0:T(2,128)S(1)}) custom-call(s32[1]{0:T(128)} %bitcast.3.refs_0_.within_ref, bf16[24,152,200]{2,1,0:T(8,128)(2,1)S(1)} %copy-done.2, bf16[3,152,200]{2,1,0:T(8,128)(2,1)S(1)} %collective-permute-done.refs_2_, f32[24,152,1]{2,1,0:T(8,128)S(1)} %copy.35.refs_3_.wet_ref.refs_5_, ...), custom_call_target="tpu_custom_call" | custom-call | flops 4096 | bytes 4096 | tf_op jit(solution)/shard_map/depthwiseb/pallas_call | solution.py:148
  50.7 3.6 %all-to-all-start = ((bf16[4,1432,128]{2,1,0:T(8,128)(2,1)}), bf16[4,1432,128]{2,1,0:T(8,128)(2,1)S(1)}, u32[]{:S(2)}, u32[]{:S(2)}) async-start(bf16[4,1432,128]{2,1,0:T(8,128)(2,1)} %bitcast.10), calls=%async_computation | async-start | bytes 2932736 | tf_op jit(solution)/shard_map/all_to_all | solution.py:892
  56.4 15.0 %collective-permute-done.6.refs_9_ = bf16[2552,128]{1,0:T(8,128)(2,1)S(1)} collective-permute-done((bf16[2552,128]{1,0:T(8,128)(2,1)}, bf16[2552,128]{1,0:T(8,128)(2,1)S(1)}, u32[]{:S(2)}, u32[]{:S(2)}) %collective-permute-start.6) | collective-permute-done | bytes 653344 | tf_op jit(solution)/shard_map/ppermute | solution.py:29
  75.0 4.5 %cut.1 = (bf16[5728,128]{1,0:T(8,128)(2,1)}, f32[1,200]{1,0:T(1,128)S(1)}) custom-call(bf16[24,152,200]{2,1,0:T(8,128)(2,1)S(1)} %copy-done.5, f32[24,152,1]{2,1,0:T(8,128)S(1)} %copy.35.refs_3_.wet_ref.refs_5_), custom_call_target="tpu_custom_call" | custom-call | flops 4096 | bytes 4096 | tf_op jit(solution)/shard_map/cut/pallas_call | solution.py:337
  79.5 8.2 %collective-permute-done.7.refs_6_ = bf16[2552,128]{1,0:T(8,128)(2,1)S(1)} collective-permute-done((bf16[2552,128]{1,0:T(8,128)(2,1)}, bf16[2552,128]{1,0:T(8,128)(2,1)S(1)}, u32[]{:S(2)}, u32[]{:S(2)}) %collective-permute-start.7) | collective-permute-done | bytes 653344 | tf_op jit(solution)/shard_map/ppermute | solution.py:29
  89.6 4.5 %all-to-all-start.2 = ((bf16[4,1432,128]{2,1,0:T(8,128)(2,1)}), bf16[4,1432,128]{2,1,0:T(8,128)(2,1)}, u32[]{:S(2)}, u32[]{:S(2)}) async-start(bf16[4,1432,128]{2,1,0:T(8,128)(2,1)} %bitcast.14), calls=%async_computation.2 | async-start | bytes 2932736 | tf_op jit(solution)/shard_map/all_to_all | solution.py:892
  94.2 29.5 %forward.1 = (bf16[5728,128]{1,0:T(8,128)(2,1)}, bf16[5728,128]{1,0:T(8,128)(2,1)}, bf16[2,912,1792]{2,1,0:T(8,128)(2,1)}, f32[2,912,1792]{2,1,0:T(8,128)}, bf16...) custom-call(s32[1]{0:T(128)} %bitcast.2.refs_0_.quarter_ref, bf16[5728,128]{1,0:T(8,128)(2,1)} %bitcast.43, ...), custom_call_target="tpu_custom_call" | custom-call | flops 4096 | bytes 4096 | tf_op jit(solution)/shard_map/forward/pallas_call | solution.py:640
  130.6 4.6 %all-to-all-start.1 = ((bf16[4,1432,128]{2,1,0:T(8,128)(2,1)}), bf16[4,1432,128]{2,1,0:T(8,128)(2,1)S(1)}, u32[]{:S(2)}, u32[]{:S(2)}) async-start(bf16[4,1432,128]{2,1,0:T(8,128)(2,1)} %bitcast.28), calls=%async_computation.1 | async-start | bytes 2932736 | tf_op jit(solution)/shard_map/all_to_all | solution.py:892
  135.2 24.2 %backward.1 = (bf16[5728,128]{1,0:T(8,128)(2,1)}, bf16[5728,128]{1,0:T(8,128)(2,1)}, bf16[2,912,1792]{2,1,0:T(8,128)(2,1)}, bf16[2,4,208,912]{3,2,1,0:T(8,128)(2,1)}) custom-call(bf16[5728,128]{1,0:T(8,128)(2,1)} %bitcast.15.refs_0_, bf16[5728,128]{1,0:T(8,128)(2,1)} %collective-permute-done.12.refs_1_, bf16[2,1024,1792]{2,1,0:T(8,128)(2,1)} %get-tuple-element.117.refs_2_, ...), custom_call_target="tpu_custom_call" | custom-call | flops 4096 | bytes 4096 | tf_op jit(solution)/shard_map/backward/pallas_call | solution.py:708
  159.5 11.5 %out_grads.1 = (f32[208,1792]{1,0:T(8,128)}, bf16[208,1792]{1,0:T(8,128)(2,1)}, bf16[208,1792]{1,0:T(8,128)(2,1)}, bf16[208,1792]{1,0:T(8,128)(2,1)}) custom-call(s32[1]{0:T(128)} %bitcast.2.refs_0_.quarter_ref, bf16[2,4,208,912]{3,2,1,0:T(8,128)(2,1)} %get-tuple-element.122.left_ref, bf16[2,912,1792]{2,1,0:T(8,128)(2,1)} %get-tuple-element.123.right_ref), custom_call_target="tpu_custom_call" | custom-call | flops 4096 | bytes 4096 | tf_op jit(solution)/shard_map/out_grads/pallas_call | solution.py:743
  175.2 5.1 %all-to-all-start.3 = ((bf16[4,1432,128]{2,1,0:T(8,128)(2,1)}), bf16[4,1432,128]{2,1,0:T(8,128)(2,1)}, u32[]{:S(2)}, u32[]{:S(2)}) async-start(bf16[4,1432,128]{2,1,0:T(8,128)(2,1)} %bitcast.27), calls=%async_computation.3 | async-start | bytes 2932736 | tf_op jit(solution)/shard_map/all_to_all | solution.py:892
  183.8 11.5 %in_grads.1 = (f32[208,1792]{1,0:T(8,128)}, bf16[208,1792]{1,0:T(8,128)(2,1)}, bf16[208,1792]{1,0:T(8,128)(2,1)}, bf16[208,1792]{1,0:T(8,128)(2,1)}) custom-call(s32[1]{0:T(128)} %bitcast.2.refs_0_.quarter_ref, bf16[2,4,208,912]{3,2,1,0:T(8,128)(2,1)} %get-tuple-element.114.left_ref, bf16[2,912,1792]{2,1,0:T(8,128)(2,1)} %get-tuple-element.127.right_ref), custom_call_target="tpu_custom_call" | custom-call | flops 4096 | bytes 4096 | tf_op jit(solution)/shard_map/in_grads/pallas_call | solution.py:743
  201.7 14.6 %collective-permute-done.18.refs_1_ = bf16[208,1792]{1,0:T(8,128)(2,1)} collective-permute-done((bf16[208,1792]{1,0:T(8,128)(2,1)}, bf16[208,1792]{1,0:T(8,128)(2,1)}, u32[]{:S(2)}, u32[]{:S(2)}) %collective-permute-start.18) | collective-permute-done | bytes 745504 | tf_op jit(solution)/shard_map/ppermute | solution.py:29
  220.2 3.6 %moments.1 = (f32[2,200]{1,0:T(2,128)S(1)}, bf16[4,912,200]{2,1,0:T(8,128)(2,1)S(1)}) custom-call(f32[12,152,200]{2,1,0:T(8,128)S(1)} %copy-done.8, f32[12,152,200]{2,1,0:T(8,128)S(1)} %copy-done.11, f32[2,200]{1,0:T(2,128)S(1)} %get-tuple-element.132.refs_2_, bf16[5728,128]{1,0:T(8,128)(2,1)} %bitcast.17.refs_3_), custom_call_target="tpu_custom_call" | custom-call | flops 4096 | bytes 4096 | tf_op jit(solution)/shard_map/moments/pallas_call | solution.py:406
  232.2 7.9 %depthwise_back_a.1 = (f32[24,152,200]{2,1,0:T(8,128)}, f32[49,200]{1,0:T(8,128)S(1)}) custom-call(s32[1]{0:T(128)} %bitcast.3.refs_0_.within_ref, f32[24,152,200]{2,1,0:T(8,128)S(1)} %get-tuple-element.144.refs_1_, bf16[3,152,200]{2,1,0:T(8,128)(2,1)S(1)} %collective-permute-done.21.refs_2_, bf16[24,152,200]{2,1,0:T(8,128)(2,1)S(1)} %copy-done.3, ...), custom_call_target="tpu_custom_call" | custom-call | flops 4096 | bytes 4096 | tf_op jit(solution)/shard_map/depthwise_back_a/pallas_call | solution.py:218
  240.3 7.9 %depthwise_back_b.1 = (f32[24,152,200]{2,1,0:T(8,128)}, f32[49,200]{1,0:T(8,128)S(1)}) custom-call(s32[1]{0:T(128)} %bitcast.3.refs_0_.within_ref, f32[24,152,200]{2,1,0:T(8,128)S(1)} %get-tuple-element.144.refs_1_, bf16[3,152,200]{2,1,0:T(8,128)(2,1)S(1)} %collective-permute-done.21.refs_2_, ...), custom_call_target="tpu_custom_call", output_to_operand_aliasing={{0}: (8, {})} | custom-call | flops 4096 | bytes 4096 | tf_op jit(solution)/shard_map/depthwise_back_b/pallas_call | solution.py:218
  253.5 7.9 %depthwise_back_c.1 = (f32[24,152,200]{2,1,0:T(8,128)}, f32[49,200]{1,0:T(8,128)S(1)}) custom-call(s32[1]{0:T(128)} %bitcast.3.refs_0_.within_ref, f32[24,152,200]{2,1,0:T(8,128)S(1)} %get-tuple-element.144.refs_1_, bf16[3,152,200]{2,1,0:T(8,128)(2,1)S(1)} %collective-permute-done.21.refs_2_, ...), custom_call_target="tpu_custom_call", output_to_operand_aliasing={{0}: (8, {})} | custom-call | flops 4096 | bytes 4096 | tf_op jit(solution)/shard_map/depthwise_back_c/pallas_call | solution.py:218
  261.5 3.5 %collective-permute-done.23.came_ref = bf16[208,896]{1,0:T(8,128)(2,1)S(1)} collective-permute-done((bf16[208,896]{1,0:T(8,128)(2,1)S(1)}, bf16[208,896]{1,0:T(8,128)(2,1)S(1)}, u32[]{:S(2)}, u32[]{:S(2)}) %collective-permute-start.23) | collective-permute-done | bytes 372768 | tf_op jit(solution)/shard_map/ppermute | solution.py:29
  267.4 7.9 %depthwise_back_d.1 = (f32[24,152,200]{2,1,0:T(8,128)}, f32[49,200]{1,0:T(8,128)S(1)}) custom-call(s32[1]{0:T(128)} %bitcast.3.refs_0_.within_ref, f32[24,152,200]{2,1,0:T(8,128)S(1)} %get-tuple-element.144.refs_1_, bf16[3,152,200]{2,1,0:T(8,128)(2,1)S(1)} %collective-permute-done.21.refs_2_, ...), custom_call_target="tpu_custom_call", output_to_operand_aliasing={{0}: (8, {})} | custom-call | flops 4096 | bytes 4096 | tf_op jit(solution)/shard_map/depthwise_back_d/pallas_call | solution.py:218
  292.7 4.3 %finish.1 = bf16[24,152,200]{2,1,0:T(8,128)(2,1)} custom-call(bf16[24,152,200]{2,1,0:T(8,128)(2,1)S(1)} %copy-done.4, f32[24,152,1]{2,1,0:T(8,128)S(1)} %copy.35.refs_3_.wet_ref.refs_5_, f32[1,200]{1,0:T(1,128)S(1)} %compare_convert_fusion.refs_4_.refs_6_.keep_ref, f32[1,200]{1,0:T(1,128)S(1)} %bitcast.40, bf16[5728,128]{1,0:T(8,128)(2,1)S(1)} %bitcast.26), custom_call_target="tpu_custom_call" | custom-call | flops 4096 | bytes 4096 | tf_op jit(solution)/shard_map/finish/pallas_call | solution.py:470
  299.4 6.5 %collective-permute-done.31.refs_2_ = bf16[208,896]{1,0:T(8,128)(2,1)S(1)} collective-permute-done((bf16[208,896]{1,0:T(8,128)(2,1)S(1)}, bf16[208,896]{1,0:T(8,128)(2,1)S(1)}, u32[]{:S(2)}, u32[]{:S(2)}) %collective-permute-start.31) | collective-permute-done | bytes 372768 | tf_op jit(solution)/shard_map/ppermute | solution.py:29
  309.1 4.2 %gather.1 = (f32[800,800]{1,0:T(8,128)}, f32[800,800]{1,0:T(8,128)}, f32[1,800]{1,0:T(1,128)S(1)}) custom-call(s32[2]{0:T(128)S(1)} %pad_add_fusion.place_ref, bf16[208,896]{1,0:T(8,128)(2,1)S(1)} %select_select_fusion.refs_0_, bf16[208,896]{1,0:T(8,128)(2,1)S(1)} %collective-permute-done.30.refs_1_, bf16[208,896]{1,0:T(8,128)(2,1)S(1)} %collective-permute-done.31.refs_2_, ...), custom_call_target="tpu_custom_call" | custom-call | flops 4096 | bytes 4096 | tf_op jit(solution)/shard_map/gather/pallas_call | solution.py:804
  (184 shorter events, 96.2 us)
Async XLA Ops:
  3.7 22.5 %collective-permute-start.1 = (bf16[2552,128]{1,0:T(8,128)(2,1)S(1)}, bf16[2552,128]{1,0:T(8,128)(2,1)}, u32[]{:S(2)}, u32[]{:S(2)}) collective-permute-start(bf16[2552,128]{1,0:T(8,128)(2,1)S(1)} %prepare.1), channel_id=1, source_target_pairs={{0,2},{1,3},{6,4},{7,5},{8,10},{9,11},{14,12},{15,13},{16,18},{17,... | collective-permute-start | bytes 1959944 | tf_op jit(solution)/shard_map/ppermute | solution.py:40
  26.3 16.5 %collective-permute-start.2 = (bf16[2552,128]{1,0:T(8,128)(2,1)S(1)}, bf16[2552,128]{1,0:T(8,128)(2,1)S(1)}, u32[]{:S(2)}, u32[]{:S(2)}) collective-permute-start(bf16[2552,128]{1,0:T(8,128)(2,1)S(1)} %broadcast_select_fusion.refs_3_), channel_id=1, source_target_pairs={{0,1},{1,0},{2,3},{3,2},{4,5},{5,4},{6,7},{7,6},{8,9},{9,8},{10,11... | collective-permute-start | bytes 1959944 | tf_op jit(solution)/shard_map/ppermute | solution.py:29
  28.0 16.8 %collective-permute-start.3 = (bf16[2552,128]{1,0:T(8,128)(2,1)S(1)}, bf16[2552,128]{1,0:T(8,128)(2,1)S(1)}, u32[]{:S(2)}, u32[]{:S(2)}) collective-permute-start(bf16[2552,128]{1,0:T(8,128)(2,1)S(1)} %broadcast_select_fusion.refs_3_), channel_id=1, source_target_pairs={{0,8},{4,12},{8,0},{12,4},{16,24},{20,28},{24,16},{28,20},{1,9},{5... | collective-permute-start | bytes 1959944 | tf_op jit(solution)/shard_map/ppermute | solution.py:29
  29.5 17.1 %collective-permute-start.4 = (bf16[2552,128]{1,0:T(8,128)(2,1)S(1)}, bf16[2552,128]{1,0:T(8,128)(2,1)S(1)}, u32[]{:S(2)}, u32[]{:S(2)}) collective-permute-start(bf16[2552,128]{1,0:T(8,128)(2,1)S(1)} %broadcast_select_fusion.refs_3_), channel_id=1, source_target_pairs={{0,16},{4,20},{8,24},{12,28},{16,0},{20,4},{24,8},{28,12},{1,17},{... | collective-permute-start | bytes 1959944 | tf_op jit(solution)/shard_map/ppermute | solution.py:29
  50.7 38.9 %all-to-all-start = ((bf16[4,1432,128]{2,1,0:T(8,128)(2,1)}), bf16[4,1432,128]{2,1,0:T(8,128)(2,1)S(1)}, u32[]{:S(2)}, u32[]{:S(2)}) async-start(bf16[4,1432,128]{2,1,0:T(8,128)(2,1)} %bitcast.10), calls=%async_computation | async-start | bytes 2932736 | tf_op jit(solution)/shard_map/all_to_all | solution.py:892
  54.3 17.2 %collective-permute-start.6 = (bf16[2552,128]{1,0:T(8,128)(2,1)}, bf16[2552,128]{1,0:T(8,128)(2,1)S(1)}, u32[]{:S(2)}, u32[]{:S(2)}) collective-permute-start(bf16[2552,128]{1,0:T(8,128)(2,1)} %copy-done.25), channel_id=1, source_target_pairs={{0,16},{4,20},{8,24},{12,28},{16,0},{20,4},{24,8},{28,12},{1,17},{... | collective-permute-start | bytes 1959944 | tf_op jit(solution)/shard_map/ppermute | solution.py:29
  55.8 23.7 %collective-permute-start.8 = (bf16[2552,128]{1,0:T(8,128)(2,1)}, bf16[2552,128]{1,0:T(8,128)(2,1)S(1)}, u32[]{:S(2)}, u32[]{:S(2)}) collective-permute-start(bf16[2552,128]{1,0:T(8,128)(2,1)} %copy-done.25), channel_id=1, source_target_pairs={{0,8},{4,12},{8,0},{12,4},{16,24},{20,28},{24,16},{28,20},{1,9},{5... | collective-permute-start | bytes 1959944 | tf_op jit(solution)/shard_map/ppermute | solution.py:29
  71.4 16.3 %collective-permute-start.7 = (bf16[2552,128]{1,0:T(8,128)(2,1)}, bf16[2552,128]{1,0:T(8,128)(2,1)S(1)}, u32[]{:S(2)}, u32[]{:S(2)}) collective-permute-start(bf16[2552,128]{1,0:T(8,128)(2,1)} %copy-done.26), channel_id=1, source_target_pairs={{0,16},{4,20},{8,24},{12,28},{16,0},{20,4},{24,8},{28,12},{1,17},{... | collective-permute-start | bytes 1959944 | tf_op jit(solution)/shard_map/ppermute | solution.py:29
  72.9 15.9 %collective-permute-start.9 = (bf16[2552,128]{1,0:T(8,128)(2,1)S(1)}, bf16[2552,128]{1,0:T(8,128)(2,1)}, u32[]{:S(2)}, u32[]{:S(2)}) collective-permute-start(bf16[2552,128]{1,0:T(8,128)(2,1)S(1)} %collective-permute-done.6.refs_9_), channel_id=1, source_target_pairs={{0,8},{4,12},{8,0},{12,4},{16,24},{20,28},{24,16},{28,20},{1,9},{5... | collective-permute-start | bytes 1959944 | tf_op jit(solution)/shard_map/ppermute | solution.py:29
  89.6 40.6 %all-to-all-start.2 = ((bf16[4,1432,128]{2,1,0:T(8,128)(2,1)}), bf16[4,1432,128]{2,1,0:T(8,128)(2,1)}, u32[]{:S(2)}, u32[]{:S(2)}) async-start(bf16[4,1432,128]{2,1,0:T(8,128)(2,1)} %bitcast.14), calls=%async_computation.2 | async-start | bytes 2932736 | tf_op jit(solution)/shard_map/all_to_all | solution.py:892
  130.6 40.4 %all-to-all-start.1 = ((bf16[4,1432,128]{2,1,0:T(8,128)(2,1)}), bf16[4,1432,128]{2,1,0:T(8,128)(2,1)S(1)}, u32[]{:S(2)}, u32[]{:S(2)}) async-start(bf16[4,1432,128]{2,1,0:T(8,128)(2,1)} %bitcast.28), calls=%async_computation.1 | async-start | bytes 2932736 | tf_op jit(solution)/shard_map/all_to_all | solution.py:892
  175.2 41.9 %all-to-all-start.3 = ((bf16[4,1432,128]{2,1,0:T(8,128)(2,1)}), bf16[4,1432,128]{2,1,0:T(8,128)(2,1)}, u32[]{:S(2)}, u32[]{:S(2)}) async-start(bf16[4,1432,128]{2,1,0:T(8,128)(2,1)} %bitcast.27), calls=%async_computation.3 | async-start | bytes 2932736 | tf_op jit(solution)/shard_map/all_to_all | solution.py:892
  180.3 19.8 %collective-permute-start.17 = (bf16[208,1792]{1,0:T(8,128)(2,1)}, bf16[208,1792]{1,0:T(8,128)(2,1)}, u32[]{:S(2)}, u32[]{:S(2)}) collective-permute-start(bf16[208,1792]{1,0:T(8,128)(2,1)} %get-tuple-element.133), channel_id=1, source_target_pairs={{0,8},{4,12},{8,0},{12,4},{16,24},{20,28},{24,16},{28,20},{1,9},{5... | collective-permute-start | bytes 2236424 | tf_op jit(solution)/shard_map/ppermute | solution.py:29
  180.9 35.4 %collective-permute-start.18 = (bf16[208,1792]{1,0:T(8,128)(2,1)}, bf16[208,1792]{1,0:T(8,128)(2,1)}, u32[]{:S(2)}, u32[]{:S(2)}) collective-permute-start(bf16[208,1792]{1,0:T(8,128)(2,1)} %get-tuple-element.134), channel_id=1, source_target_pairs={{0,16},{4,20},{8,24},{12,28},{16,0},{20,4},{24,8},{28,12},{1,17},{... | collective-permute-start | bytes 2236424 | tf_op jit(solution)/shard_map/ppermute | solution.py:29
  182.4 34.7 %collective-permute-start.19 = (bf16[208,1792]{1,0:T(8,128)(2,1)}, bf16[208,1792]{1,0:T(8,128)(2,1)}, u32[]{:S(2)}, u32[]{:S(2)}) collective-permute-start(bf16[208,1792]{1,0:T(8,128)(2,1)} %get-tuple-element.135), channel_id=1, source_target_pairs={{0,24},{4,28},{8,16},{12,20},{16,8},{20,12},{24,0},{28,4},{1,25},{... | collective-permute-start | bytes 2236424 | tf_op jit(solution)/shard_map/ppermute | solution.py:29
  195.4 52.9 %collective-permute-start.14 = (bf16[208,1792]{1,0:T(8,128)(2,1)}, bf16[208,1792]{1,0:T(8,128)(2,1)}, u32[]{:S(2)}, u32[]{:S(2)}) collective-permute-start(bf16[208,1792]{1,0:T(8,128)(2,1)} %get-tuple-element.129), channel_id=1, source_target_pairs={{0,8},{4,12},{8,0},{12,4},{16,24},{20,28},{24,16},{28,20},{1,9},{5... | collective-permute-start | bytes 2236424 | tf_op jit(solution)/shard_map/ppermute | solution.py:29
  195.9 52.3 %collective-permute-start.15 = (bf16[208,1792]{1,0:T(8,128)(2,1)}, bf16[208,1792]{1,0:T(8,128)(2,1)}, u32[]{:S(2)}, u32[]{:S(2)}) collective-permute-start(bf16[208,1792]{1,0:T(8,128)(2,1)} %get-tuple-element.130), channel_id=1, source_target_pairs={{0,16},{4,20},{8,24},{12,28},{16,0},{20,4},{24,8},{28,12},{1,17},{... | collective-permute-start | bytes 2236424 | tf_op jit(solution)/shard_map/ppermute | solution.py:29
  200.2 48.2 %collective-permute-start.16 = (bf16[208,1792]{1,0:T(8,128)(2,1)}, bf16[208,1792]{1,0:T(8,128)(2,1)}, u32[]{:S(2)}, u32[]{:S(2)}) collective-permute-start(bf16[208,1792]{1,0:T(8,128)(2,1)} %get-tuple-element.131), channel_id=1, source_target_pairs={{0,24},{4,28},{8,16},{12,20},{16,8},{20,12},{24,0},{28,4},{1,25},{... | collective-permute-start | bytes 2236424 | tf_op jit(solution)/shard_map/ppermute | solution.py:29
  250.3 14.7 %collective-permute-start.23 = (bf16[208,896]{1,0:T(8,128)(2,1)S(1)}, bf16[208,896]{1,0:T(8,128)(2,1)S(1)}, u32[]{:S(2)}, u32[]{:S(2)}) collective-permute-start(bf16[208,896]{1,0:T(8,128)(2,1)S(1)} %get-tuple-element.163), channel_id=1, source_target_pairs={{0,1},{1,0},{2,3},{3,2},{4,5},{5,4},{6,7},{7,6},{8,9},{9,8},{10,11... | collective-permute-start | bytes 1118216 | tf_op jit(solution)/shard_map/ppermute | solution.py:29
  252.2 14.2 %collective-permute-start.25 = (bf16[208,896]{1,0:T(8,128)(2,1)S(1)}, bf16[208,896]{1,0:T(8,128)(2,1)S(1)}, u32[]{:S(2)}, u32[]{:S(2)}) collective-permute-start(bf16[208,896]{1,0:T(8,128)(2,1)S(1)} %get-tuple-element.155), channel_id=1, source_target_pairs={{2,0},{3,1},{4,6},{5,7},{10,8},{11,9},{12,14},{13,15},{18,16},{19,... | collective-permute-start | bytes 1118216 | tf_op jit(solution)/shard_map/ppermute | solution.py:40
  265.1 13.6 %collective-permute-start.24 = (bf16[208,896]{1,0:T(8,128)(2,1)S(1)}, bf16[208,896]{1,0:T(8,128)(2,1)S(1)}, u32[]{:S(2)}, u32[]{:S(2)}) collective-permute-start(bf16[208,896]{1,0:T(8,128)(2,1)S(1)} %get-tuple-element.169), channel_id=1, source_target_pairs={{2,0},{3,1},{4,6},{5,7},{10,8},{11,9},{12,14},{13,15},{18,16},{19,... | collective-permute-start | bytes 1118216 | tf_op jit(solution)/shard_map/ppermute | solution.py:40
  287.7 11.7 %collective-permute-start.30 = (bf16[208,896]{1,0:T(8,128)(2,1)S(1)}, bf16[208,896]{1,0:T(8,128)(2,1)S(1)}, u32[]{:S(2)}, u32[]{:S(2)}) collective-permute-start(bf16[208,896]{1,0:T(8,128)(2,1)S(1)} %select_select_fusion.refs_0_), channel_id=1, source_target_pairs={{0,8},{4,12},{8,0},{12,4},{16,24},{20,28},{24,16},{28,20},{1,9},{5... | collective-permute-start | bytes 1118216 | tf_op jit(solution)/shard_map/ppermute | solution.py:29
  288.5 17.4 %collective-permute-start.31 = (bf16[208,896]{1,0:T(8,128)(2,1)S(1)}, bf16[208,896]{1,0:T(8,128)(2,1)S(1)}, u32[]{:S(2)}, u32[]{:S(2)}) collective-permute-start(bf16[208,896]{1,0:T(8,128)(2,1)S(1)} %select_select_fusion.refs_0_), channel_id=1, source_target_pairs={{0,16},{4,20},{8,24},{12,28},{16,0},{20,4},{24,8},{28,12},{1,17},{... | collective-permute-start | bytes 1118216 | tf_op jit(solution)/shard_map/ppermute | solution.py:29
  290.0 15.8 %collective-permute-start.32 = (bf16[208,896]{1,0:T(8,128)(2,1)S(1)}, bf16[208,896]{1,0:T(8,128)(2,1)S(1)}, u32[]{:S(2)}, u32[]{:S(2)}) collective-permute-start(bf16[208,896]{1,0:T(8,128)(2,1)S(1)} %select_select_fusion.refs_0_), channel_id=1, source_target_pairs={{0,24},{4,28},{8,16},{12,20},{16,8},{20,12},{24,0},{28,4},{1,25},{... | collective-permute-start | bytes 1118216 | tf_op jit(solution)/shard_map/ppermute | solution.py:29
  (53 other events, 311.5 us)
where the time goes:
time: 316 us; the launch traced here: 315 us
  Pallas kernels  158 us (50%)
  waiting for transfers between devices  75.6 us (24%)
  starting transfers between devices  56.2 us (18%)
  local copies, waits for them, and re-layouts  18.2 us (6%)
  other arithmetic  5.83 us (2%)
    ppermute x34, waiting for transfers between devices, flipped(): lax.ppermute(block, axis, [(place, place ^ bit) for place in range(count)])  71.4 us
    pallas_call x4, Pallas kernels, depthwise_back(): pl.pallas_call(kernel, grid=(1,), out_shape=(jax.ShapeDtypeStruct(x.shape...  31.8 us
    pallas_call x1, Pallas kernels, forward(): pl.pallas_call(kernel, grid=(2 * CHUNKS,), out_shape=(jax.ShapeDtypeStruc...  29.5 us
    ppermute x34, starting transfers between devices, flipped(): lax.ppermute(block, axis, [(place, place ^ bit) for place in range(count)])  29 us
    pallas_call x1, Pallas kernels, backward(): pl.pallas_call(backward_kernel, grid=(2 * CHUNKS,), out_shape=(jax.ShapeD...  24.2 us
    pallas_call x2, Pallas kernels, weight_grads(): pl.pallas_call(weight_grads_kernel, grid=(lanes // TILE,), out_shape=(jax...  23.1 us
    pallas_call x2, Pallas kernels, depthwise(): pl.pallas_call(kernel, out_shape=(jax.ShapeDtypeStruct((rows, across, cha...  20.1 us
    all_to_all x4, starting transfers between devices, body(): exchanged = lambda cells: lax.all_to_all(cells, 'chan', 0, 0, tiled=True)  17.7 us
  transfers between devices with their start and end apart: 41, of which 23 were waited for; matrix products, arithmetic and copies ran while one was open for 1% of the time, Pallas kernels for 48%

commit v1 on v0

--- a/solution.py
+++ b/solution.py
@@ -940,12 +940,11 @@
         [grad_taps, grad_conv_bias, sums[1:2], sums[0:1], grad_bias_out, jnp.zeros((3, channels), F32)]
     )
     bit = 1
+    output = finish(inputs, wet, keep, row(bias_out), after(branch, share))
     while 2 * bit < lax.axis_size("dp"):
-        small = small + flipped(small, "dp", bit)
+        small = small + (after(flipped(small, "dp", bit), output) if bit > 1 else flipped(small, "dp", bit))
         bit *= 2
-    share = after(share, small)
-    output = finish(inputs, wet, keep, row(bias_out), after(branch, share))
-    shares = after([share] + [flipped(share, "dp", SPAN * j) for j in range(1, PARTS)], output)
+    shares = after([share] + [flipped(share, "dp", SPAN * j) for j in range(1, PARTS)], (output, small))
     grad_weight_in, grad_weight_out, grad_bias_in = gather(
         jnp.stack([core, quarter]).astype(jnp.int32), shares, [other_core(value) for value in shares], channels, units
     )

time: 316 us -> 314 us (level)
    unnamed x73 -> x69, local copies, waits for them, and re-layouts: 15.1 us -> 15.1 us
where the time goes in v1:
time: 314 us; the launch traced here: 313 us
  Pallas kernels  159 us (51%)
  waiting for transfers between devices  74.7 us (24%)
  starting transfers between devices  55.1 us (18%)
  local copies, waits for them, and re-layouts  18.2 us (6%)
  other arithmetic  4.79 us (2%)
    ppermute x34, waiting for transfers between devices, flipped(): lax.ppermute(block, axis, [(place, place ^ bit) for place in range(count)])  70.5 us
    pallas_call x4, Pallas kernels, depthwise_back(): pl.pallas_call(kernel, grid=(1,), out_shape=(jax.ShapeDtypeStruct(x.shape...  31.8 us
    pallas_call x1, Pallas kernels, forward(): pl.pallas_call(kernel, grid=(2 * CHUNKS,), out_shape=(jax.ShapeDtypeStruc...  29.6 us
    ppermute x34, starting transfers between devices, flipped(): lax.ppermute(block, axis, [(place, place ^ bit) for place in range(count)])  27.9 us
    pallas_call x1, Pallas kernels, backward(): pl.pallas_call(backward_kernel, grid=(2 * CHUNKS,), out_shape=(jax.ShapeD...  24.2 us
    pallas_call x2, Pallas kernels, weight_grads(): pl.pallas_call(weight_grads_kernel, grid=(lanes // TILE,), out_shape=(jax...  23.1 us
    pallas_call x2, Pallas kernels, depthwise(): pl.pallas_call(kernel, out_shape=(jax.ShapeDtypeStruct((rows, across, cha...  20.1 us
    all_to_all x4, starting transfers between devices, body(): exchanged = lambda cells: lax.all_to_all(cells, 'chan', 0, 0, tiled=True)  17.7 us
  transfers between devices with their start and end apart: 41, of which 23 were waited for; matrix products, arithmetic and copies ran while one was open for 1% of the time, Pallas kernels for 48%

profile of v1, /device:TPU:0, one launch (start us, length us, event | category | flops | bytes accessed | tf_op | source)
XLA Modules:
  0.0 313.0 jit_solution(11526485259147085466)
XLA Ops:
  3.7 6.9 %collective-permute-start.1 = (bf16[2552,128]{1,0:T(8,128)(2,1)S(1)}, bf16[2552,128]{1,0:T(8,128)(2,1)}, u32[]{:S(2)}, u32[]{:S(2)}) collective-permute-start(bf16[2552,128]{1,0:T(8,128)(2,1)S(1)} %prepare.1), channel_id=1, source_target_pairs={{0,2},{1,3},{6,4},{7,5},{8,10},{9,11},{14,12},{15,13},{16,18},{17,... | collective-permute-start | bytes 1959944 | tf_op jit(solution)/shard_map/ppermute | solution.py:40
  16.1 10.0 %depthwisea.1 = (f32[12,152,200]{2,1,0:T(8,128)S(1)}, f32[2,200]{1,0:T(2,128)S(1)}) custom-call(s32[1]{0:T(128)} %bitcast.3.refs_0_.within_ref, bf16[24,152,200]{2,1,0:T(8,128)(2,1)S(1)} %copy-done.2, bf16[3,152,200]{2,1,0:T(8,128)(2,1)S(1)} %collective-permute-done.refs_2_, f32[24,152,1]{2,1,0:T(8,128)S(1)} %copy.35.refs_3_.wet_ref.refs_5_, ...), custom_call_target="tpu_custom_call" | custom-call | flops 4096 | bytes 4096 | tf_op jit(solution)/shard_map/depthwisea/pallas_call | solution.py:148
  31.0 10.0 %depthwiseb.1 = (f32[12,152,200]{2,1,0:T(8,128)S(1)}, f32[2,200]{1,0:T(2,128)S(1)}) custom-call(s32[1]{0:T(128)} %bitcast.3.refs_0_.within_ref, bf16[24,152,200]{2,1,0:T(8,128)(2,1)S(1)} %copy-done.2, bf16[3,152,200]{2,1,0:T(8,128)(2,1)S(1)} %collective-permute-done.refs_2_, f32[24,152,1]{2,1,0:T(8,128)S(1)} %copy.35.refs_3_.wet_ref.refs_5_, ...), custom_call_target="tpu_custom_call" | custom-call | flops 4096 | bytes 4096 | tf_op jit(solution)/shard_map/depthwiseb/pallas_call | solution.py:148
  50.7 3.6 %all-to-all-start = ((bf16[4,1432,128]{2,1,0:T(8,128)(2,1)}), bf16[4,1432,128]{2,1,0:T(8,128)(2,1)S(1)}, u32[]{:S(2)}, u32[]{:S(2)}) async-start(bf16[4,1432,128]{2,1,0:T(8,128)(2,1)} %bitcast.10), calls=%async_computation | async-start | bytes 2932736 | tf_op jit(solution)/shard_map/all_to_all | solution.py:892
  56.4 15.0 %collective-permute-done.6.refs_9_ = bf16[2552,128]{1,0:T(8,128)(2,1)S(1)} collective-permute-done((bf16[2552,128]{1,0:T(8,128)(2,1)}, bf16[2552,128]{1,0:T(8,128)(2,1)S(1)}, u32[]{:S(2)}, u32[]{:S(2)}) %collective-permute-start.6) | collective-permute-done | bytes 653344 | tf_op jit(solution)/shard_map/ppermute | solution.py:29
  75.0 4.5 %cut.1 = (bf16[5728,128]{1,0:T(8,128)(2,1)}, f32[1,200]{1,0:T(1,128)S(1)}) custom-call(bf16[24,152,200]{2,1,0:T(8,128)(2,1)S(1)} %copy-done.5, f32[24,152,1]{2,1,0:T(8,128)S(1)} %copy.35.refs_3_.wet_ref.refs_5_), custom_call_target="tpu_custom_call" | custom-call | flops 4096 | bytes 4096 | tf_op jit(solution)/shard_map/cut/pallas_call | solution.py:337
  79.5 8.2 %collective-permute-done.7.refs_6_ = bf16[2552,128]{1,0:T(8,128)(2,1)S(1)} collective-permute-done((bf16[2552,128]{1,0:T(8,128)(2,1)}, bf16[2552,128]{1,0:T(8,128)(2,1)S(1)}, u32[]{:S(2)}, u32[]{:S(2)}) %collective-permute-start.7) | collective-permute-done | bytes 653344 | tf_op jit(solution)/shard_map/ppermute | solution.py:29
  89.6 4.5 %all-to-all-start.2 = ((bf16[4,1432,128]{2,1,0:T(8,128)(2,1)}), bf16[4,1432,128]{2,1,0:T(8,128)(2,1)}, u32[]{:S(2)}, u32[]{:S(2)}) async-start(bf16[4,1432,128]{2,1,0:T(8,128)(2,1)} %bitcast.14), calls=%async_computation.2 | async-start | bytes 2932736 | tf_op jit(solution)/shard_map/all_to_all | solution.py:892
  94.2 29.6 %forward.1 = (bf16[5728,128]{1,0:T(8,128)(2,1)}, bf16[5728,128]{1,0:T(8,128)(2,1)}, bf16[2,912,1792]{2,1,0:T(8,128)(2,1)}, f32[2,912,1792]{2,1,0:T(8,128)}, bf16...) custom-call(s32[1]{0:T(128)} %bitcast.2.refs_0_.quarter_ref, bf16[5728,128]{1,0:T(8,128)(2,1)} %bitcast.43, ...), custom_call_target="tpu_custom_call" | custom-call | flops 4096 | bytes 4096 | tf_op jit(solution)/shard_map/forward/pallas_call | solution.py:640
  130.7 4.6 %all-to-all-start.1 = ((bf16[4,1432,128]{2,1,0:T(8,128)(2,1)}), bf16[4,1432,128]{2,1,0:T(8,128)(2,1)S(1)}, u32[]{:S(2)}, u32[]{:S(2)}) async-start(bf16[4,1432,128]{2,1,0:T(8,128)(2,1)} %bitcast.28), calls=%async_computation.1 | async-start | bytes 2932736 | tf_op jit(solution)/shard_map/all_to_all | solution.py:892
  135.2 24.2 %backward.1 = (bf16[5728,128]{1,0:T(8,128)(2,1)}, bf16[5728,128]{1,0:T(8,128)(2,1)}, bf16[2,912,1792]{2,1,0:T(8,128)(2,1)}, bf16[2,4,208,912]{3,2,1,0:T(8,128)(2,1)}) custom-call(bf16[5728,128]{1,0:T(8,128)(2,1)} %bitcast.15.refs_0_, bf16[5728,128]{1,0:T(8,128)(2,1)} %collective-permute-done.12.refs_1_, bf16[2,1024,1792]{2,1,0:T(8,128)(2,1)} %get-tuple-element.117.refs_2_, ...), custom_call_target="tpu_custom_call" | custom-call | flops 4096 | bytes 4096 | tf_op jit(solution)/shard_map/backward/pallas_call | solution.py:708
  159.6 11.5 %out_grads.1 = (f32[208,1792]{1,0:T(8,128)}, bf16[208,1792]{1,0:T(8,128)(2,1)}, bf16[208,1792]{1,0:T(8,128)(2,1)}, bf16[208,1792]{1,0:T(8,128)(2,1)}) custom-call(s32[1]{0:T(128)} %bitcast.2.refs_0_.quarter_ref, bf16[2,4,208,912]{3,2,1,0:T(8,128)(2,1)} %get-tuple-element.122.left_ref, bf16[2,912,1792]{2,1,0:T(8,128)(2,1)} %get-tuple-element.123.right_ref), custom_call_target="tpu_custom_call" | custom-call | flops 4096 | bytes 4096 | tf_op jit(solution)/shard_map/out_grads/pallas_call | solution.py:743
  175.3 5.1 %all-to-all-start.3 = ((bf16[4,1432,128]{2,1,0:T(8,128)(2,1)}), bf16[4,1432,128]{2,1,0:T(8,128)(2,1)}, u32[]{:S(2)}, u32[]{:S(2)}) async-start(bf16[4,1432,128]{2,1,0:T(8,128)(2,1)} %bitcast.27), calls=%async_computation.3 | async-start | bytes 2932736 | tf_op jit(solution)/shard_map/all_to_all | solution.py:892
  183.9 11.6 %in_grads.1 = (f32[208,1792]{1,0:T(8,128)}, bf16[208,1792]{1,0:T(8,128)(2,1)}, bf16[208,1792]{1,0:T(8,128)(2,1)}, bf16[208,1792]{1,0:T(8,128)(2,1)}) custom-call(s32[1]{0:T(128)} %bitcast.2.refs_0_.quarter_ref, bf16[2,4,208,912]{3,2,1,0:T(8,128)(2,1)} %get-tuple-element.114.left_ref, bf16[2,912,1792]{2,1,0:T(8,128)(2,1)} %get-tuple-element.127.right_ref), custom_call_target="tpu_custom_call" | custom-call | flops 4096 | bytes 4096 | tf_op jit(solution)/shard_map/in_grads/pallas_call | solution.py:743
  201.7 14.6 %collective-permute-done.18.refs_1_ = bf16[208,1792]{1,0:T(8,128)(2,1)} collective-permute-done((bf16[208,1792]{1,0:T(8,128)(2,1)}, bf16[208,1792]{1,0:T(8,128)(2,1)}, u32[]{:S(2)}, u32[]{:S(2)}) %collective-permute-start.18) | collective-permute-done | bytes 745504 | tf_op jit(solution)/shard_map/ppermute | solution.py:29
  220.2 3.6 %moments.1 = (f32[2,200]{1,0:T(2,128)S(1)}, bf16[4,912,200]{2,1,0:T(8,128)(2,1)S(1)}) custom-call(f32[12,152,200]{2,1,0:T(8,128)S(1)} %copy-done.8, f32[12,152,200]{2,1,0:T(8,128)S(1)} %copy-done.11, f32[2,200]{1,0:T(2,128)S(1)} %get-tuple-element.132.refs_2_, bf16[5728,128]{1,0:T(8,128)(2,1)} %bitcast.17.refs_3_), custom_call_target="tpu_custom_call" | custom-call | flops 4096 | bytes 4096 | tf_op jit(solution)/shard_map/moments/pallas_call | solution.py:406
  232.2 7.9 %depthwise_back_a.1 = (f32[24,152,200]{2,1,0:T(8,128)}, f32[49,200]{1,0:T(8,128)S(1)}) custom-call(s32[1]{0:T(128)} %bitcast.3.refs_0_.within_ref, f32[24,152,200]{2,1,0:T(8,128)S(1)} %get-tuple-element.144.refs_1_, bf16[3,152,200]{2,1,0:T(8,128)(2,1)S(1)} %collective-permute-done.21.refs_2_, bf16[24,152,200]{2,1,0:T(8,128)(2,1)S(1)} %copy-done.3, ...), custom_call_target="tpu_custom_call" | custom-call | flops 4096 | bytes 4096 | tf_op jit(solution)/shard_map/depthwise_back_a/pallas_call | solution.py:218
  240.3 7.9 %depthwise_back_b.1 = (f32[24,152,200]{2,1,0:T(8,128)}, f32[49,200]{1,0:T(8,128)S(1)}) custom-call(s32[1]{0:T(128)} %bitcast.3.refs_0_.within_ref, f32[24,152,200]{2,1,0:T(8,128)S(1)} %get-tuple-element.144.refs_1_, bf16[3,152,200]{2,1,0:T(8,128)(2,1)S(1)} %collective-permute-done.21.refs_2_, ...), custom_call_target="tpu_custom_call", output_to_operand_aliasing={{0}: (8, {})} | custom-call | flops 4096 | bytes 4096 | tf_op jit(solution)/shard_map/depthwise_back_b/pallas_call | solution.py:218
  253.5 7.9 %depthwise_back_c.1 = (f32[24,152,200]{2,1,0:T(8,128)}, f32[49,200]{1,0:T(8,128)S(1)}) custom-call(s32[1]{0:T(128)} %bitcast.3.refs_0_.within_ref, f32[24,152,200]{2,1,0:T(8,128)S(1)} %get-tuple-element.144.refs_1_, bf16[3,152,200]{2,1,0:T(8,128)(2,1)S(1)} %collective-permute-done.21.refs_2_, ...), custom_call_target="tpu_custom_call", output_to_operand_aliasing={{0}: (8, {})} | custom-call | flops 4096 | bytes 4096 | tf_op jit(solution)/shard_map/depthwise_back_c/pallas_call | solution.py:218
  261.5 3.5 %collective-permute-done.23.came_ref = bf16[208,896]{1,0:T(8,128)(2,1)S(1)} collective-permute-done((bf16[208,896]{1,0:T(8,128)(2,1)S(1)}, bf16[208,896]{1,0:T(8,128)(2,1)S(1)}, u32[]{:S(2)}, u32[]{:S(2)}) %collective-permute-start.23) | collective-permute-done | bytes 372768 | tf_op jit(solution)/shard_map/ppermute | solution.py:29
  267.4 7.9 %depthwise_back_d.1 = (f32[24,152,200]{2,1,0:T(8,128)}, f32[49,200]{1,0:T(8,128)S(1)}) custom-call(s32[1]{0:T(128)} %bitcast.3.refs_0_.within_ref, f32[24,152,200]{2,1,0:T(8,128)S(1)} %get-tuple-element.144.refs_1_, bf16[3,152,200]{2,1,0:T(8,128)(2,1)S(1)} %collective-permute-done.21.refs_2_, ...), custom_call_target="tpu_custom_call", output_to_operand_aliasing={{0}: (8, {})} | custom-call | flops 4096 | bytes 4096 | tf_op jit(solution)/shard_map/depthwise_back_d/pallas_call | solution.py:218
  289.6 4.3 %finish.1 = bf16[24,152,200]{2,1,0:T(8,128)(2,1)} custom-call(bf16[24,152,200]{2,1,0:T(8,128)(2,1)S(1)} %copy-done.4, f32[24,152,1]{2,1,0:T(8,128)S(1)} %copy.35.refs_3_.wet_ref.refs_5_, f32[1,200]{1,0:T(1,128)S(1)} %compare_convert_fusion.refs_4_.refs_6_.keep_ref, f32[1,200]{1,0:T(1,128)S(1)} %bitcast.40, bf16[5728,128]{1,0:T(8,128)(2,1)S(1)} %bitcast.26), custom_call_target="tpu_custom_call" | custom-call | flops 4096 | bytes 4096 | tf_op jit(solution)/shard_map/finish/pallas_call | solution.py:470
  293.9 8.6 %collective-permute-done.28 = f32[56,200]{1,0:T(8,128)S(1)} collective-permute-done((f32[56,200]{1,0:T(8,128)S(1)}, f32[56,200]{1,0:T(8,128)S(1)}, u32[]{:S(2)}, u32[]{:S(2)}) %collective-permute-start.28) | collective-permute-done | bytes 44832 | tf_op jit(solution)/shard_map/ppermute | solution.py:29
  306.1 5.0 %gather.1 = (f32[800,800]{1,0:T(8,128)}, f32[800,800]{1,0:T(8,128)}, f32[1,800]{1,0:T(1,128)S(1)}) custom-call(s32[2]{0:T(128)S(1)} %pad_add_fusion.place_ref, bf16[208,896]{1,0:T(8,128)(2,1)} %select_select_fusion.refs_0_, bf16[208,896]{1,0:T(8,128)(2,1)} %collective-permute-done.30.refs_1_, bf16[208,896]{1,0:T(8,128)(2,1)} %collective-permute-done.31.refs_2_, ...), custom_call_target="tpu_custom_call" | custom-call | flops 4096 | bytes 4096 | tf_op jit(solution)/shard_map/gather/pallas_call | solution.py:804
  (180 shorter events, 90.9 us)
Async XLA Ops:
  3.7 22.4 %collective-permute-start.1 = (bf16[2552,128]{1,0:T(8,128)(2,1)S(1)}, bf16[2552,128]{1,0:T(8,128)(2,1)}, u32[]{:S(2)}, u32[]{:S(2)}) collective-permute-start(bf16[2552,128]{1,0:T(8,128)(2,1)S(1)} %prepare.1), channel_id=1, source_target_pairs={{0,2},{1,3},{6,4},{7,5},{8,10},{9,11},{14,12},{15,13},{16,18},{17,... | collective-permute-start | bytes 1959944 | tf_op jit(solution)/shard_map/ppermute | solution.py:40
  26.3 16.5 %collective-permute-start.2 = (bf16[2552,128]{1,0:T(8,128)(2,1)S(1)}, bf16[2552,128]{1,0:T(8,128)(2,1)S(1)}, u32[]{:S(2)}, u32[]{:S(2)}) collective-permute-start(bf16[2552,128]{1,0:T(8,128)(2,1)S(1)} %broadcast_select_fusion.refs_3_), channel_id=1, source_target_pairs={{0,1},{1,0},{2,3},{3,2},{4,5},{5,4},{6,7},{7,6},{8,9},{9,8},{10,11... | collective-permute-start | bytes 1959944 | tf_op jit(solution)/shard_map/ppermute | solution.py:29
  28.0 16.8 %collective-permute-start.3 = (bf16[2552,128]{1,0:T(8,128)(2,1)S(1)}, bf16[2552,128]{1,0:T(8,128)(2,1)S(1)}, u32[]{:S(2)}, u32[]{:S(2)}) collective-permute-start(bf16[2552,128]{1,0:T(8,128)(2,1)S(1)} %broadcast_select_fusion.refs_3_), channel_id=1, source_target_pairs={{0,8},{4,12},{8,0},{12,4},{16,24},{20,28},{24,16},{28,20},{1,9},{5... | collective-permute-start | bytes 1959944 | tf_op jit(solution)/shard_map/ppermute | solution.py:29
  29.5 17.1 %collective-permute-start.4 = (bf16[2552,128]{1,0:T(8,128)(2,1)S(1)}, bf16[2552,128]{1,0:T(8,128)(2,1)S(1)}, u32[]{:S(2)}, u32[]{:S(2)}) collective-permute-start(bf16[2552,128]{1,0:T(8,128)(2,1)S(1)} %broadcast_select_fusion.refs_3_), channel_id=1, source_target_pairs={{0,16},{4,20},{8,24},{12,28},{16,0},{20,4},{24,8},{28,12},{1,17},{... | collective-permute-start | bytes 1959944 | tf_op jit(solution)/shard_map/ppermute | solution.py:29
  50.7 38.9 %all-to-all-start = ((bf16[4,1432,128]{2,1,0:T(8,128)(2,1)}), bf16[4,1432,128]{2,1,0:T(8,128)(2,1)S(1)}, u32[]{:S(2)}, u32[]{:S(2)}) async-start(bf16[4,1432,128]{2,1,0:T(8,128)(2,1)} %bitcast.10), calls=%async_computation | async-start | bytes 2932736 | tf_op jit(solution)/shard_map/all_to_all | solution.py:892
  54.2 17.2 %collective-permute-start.6 = (bf16[2552,128]{1,0:T(8,128)(2,1)}, bf16[2552,128]{1,0:T(8,128)(2,1)S(1)}, u32[]{:S(2)}, u32[]{:S(2)}) collective-permute-start(bf16[2552,128]{1,0:T(8,128)(2,1)} %copy-done.23), channel_id=1, source_target_pairs={{0,16},{4,20},{8,24},{12,28},{16,0},{20,4},{24,8},{28,12},{1,17},{... | collective-permute-start | bytes 1959944 | tf_op jit(solution)/shard_map/ppermute | solution.py:29
  55.8 23.6 %collective-permute-start.8 = (bf16[2552,128]{1,0:T(8,128)(2,1)}, bf16[2552,128]{1,0:T(8,128)(2,1)S(1)}, u32[]{:S(2)}, u32[]{:S(2)}) collective-permute-start(bf16[2552,128]{1,0:T(8,128)(2,1)} %copy-done.23), channel_id=1, source_target_pairs={{0,8},{4,12},{8,0},{12,4},{16,24},{20,28},{24,16},{28,20},{1,9},{5... | collective-permute-start | bytes 1959944 | tf_op jit(solution)/shard_map/ppermute | solution.py:29
  71.4 16.3 %collective-permute-start.7 = (bf16[2552,128]{1,0:T(8,128)(2,1)}, bf16[2552,128]{1,0:T(8,128)(2,1)S(1)}, u32[]{:S(2)}, u32[]{:S(2)}) collective-permute-start(bf16[2552,128]{1,0:T(8,128)(2,1)} %copy-done.24), channel_id=1, source_target_pairs={{0,16},{4,20},{8,24},{12,28},{16,0},{20,4},{24,8},{28,12},{1,17},{... | collective-permute-start | bytes 1959944 | tf_op jit(solution)/shard_map/ppermute | solution.py:29
  72.9 15.9 %collective-permute-start.9 = (bf16[2552,128]{1,0:T(8,128)(2,1)S(1)}, bf16[2552,128]{1,0:T(8,128)(2,1)}, u32[]{:S(2)}, u32[]{:S(2)}) collective-permute-start(bf16[2552,128]{1,0:T(8,128)(2,1)S(1)} %collective-permute-done.6.refs_9_), channel_id=1, source_target_pairs={{0,8},{4,12},{8,0},{12,4},{16,24},{20,28},{24,16},{28,20},{1,9},{5... | collective-permute-start | bytes 1959944 | tf_op jit(solution)/shard_map/ppermute | solution.py:29
  89.6 40.7 %all-to-all-start.2 = ((bf16[4,1432,128]{2,1,0:T(8,128)(2,1)}), bf16[4,1432,128]{2,1,0:T(8,128)(2,1)}, u32[]{:S(2)}, u32[]{:S(2)}) async-start(bf16[4,1432,128]{2,1,0:T(8,128)(2,1)} %bitcast.14), calls=%async_computation.2 | async-start | bytes 2932736 | tf_op jit(solution)/shard_map/all_to_all | solution.py:892
  130.7 40.4 %all-to-all-start.1 = ((bf16[4,1432,128]{2,1,0:T(8,128)(2,1)}), bf16[4,1432,128]{2,1,0:T(8,128)(2,1)S(1)}, u32[]{:S(2)}, u32[]{:S(2)}) async-start(bf16[4,1432,128]{2,1,0:T(8,128)(2,1)} %bitcast.28), calls=%async_computation.1 | async-start | bytes 2932736 | tf_op jit(solution)/shard_map/all_to_all | solution.py:892
  175.3 41.9 %all-to-all-start.3 = ((bf16[4,1432,128]{2,1,0:T(8,128)(2,1)}), bf16[4,1432,128]{2,1,0:T(8,128)(2,1)}, u32[]{:S(2)}, u32[]{:S(2)}) async-start(bf16[4,1432,128]{2,1,0:T(8,128)(2,1)} %bitcast.27), calls=%async_computation.3 | async-start | bytes 2932736 | tf_op jit(solution)/shard_map/all_to_all | solution.py:892
  180.4 19.8 %collective-permute-start.17 = (bf16[208,1792]{1,0:T(8,128)(2,1)}, bf16[208,1792]{1,0:T(8,128)(2,1)}, u32[]{:S(2)}, u32[]{:S(2)}) collective-permute-start(bf16[208,1792]{1,0:T(8,128)(2,1)} %get-tuple-element.133), channel_id=1, source_target_pairs={{0,8},{4,12},{8,0},{12,4},{16,24},{20,28},{24,16},{28,20},{1,9},{5... | collective-permute-start | bytes 2236424 | tf_op jit(solution)/shard_map/ppermute | solution.py:29
  180.9 35.4 %collective-permute-start.18 = (bf16[208,1792]{1,0:T(8,128)(2,1)}, bf16[208,1792]{1,0:T(8,128)(2,1)}, u32[]{:S(2)}, u32[]{:S(2)}) collective-permute-start(bf16[208,1792]{1,0:T(8,128)(2,1)} %get-tuple-element.134), channel_id=1, source_target_pairs={{0,16},{4,20},{8,24},{12,28},{16,0},{20,4},{24,8},{28,12},{1,17},{... | collective-permute-start | bytes 2236424 | tf_op jit(solution)/shard_map/ppermute | solution.py:29
  182.5 34.7 %collective-permute-start.19 = (bf16[208,1792]{1,0:T(8,128)(2,1)}, bf16[208,1792]{1,0:T(8,128)(2,1)}, u32[]{:S(2)}, u32[]{:S(2)}) collective-permute-start(bf16[208,1792]{1,0:T(8,128)(2,1)} %get-tuple-element.135), channel_id=1, source_target_pairs={{0,24},{4,28},{8,16},{12,20},{16,8},{20,12},{24,0},{28,4},{1,25},{... | collective-permute-start | bytes 2236424 | tf_op jit(solution)/shard_map/ppermute | solution.py:29
  195.4 52.8 %collective-permute-start.14 = (bf16[208,1792]{1,0:T(8,128)(2,1)}, bf16[208,1792]{1,0:T(8,128)(2,1)}, u32[]{:S(2)}, u32[]{:S(2)}) collective-permute-start(bf16[208,1792]{1,0:T(8,128)(2,1)} %get-tuple-element.129), channel_id=1, source_target_pairs={{0,8},{4,12},{8,0},{12,4},{16,24},{20,28},{24,16},{28,20},{1,9},{5... | collective-permute-start | bytes 2236424 | tf_op jit(solution)/shard_map/ppermute | solution.py:29
  196.0 52.3 %collective-permute-start.15 = (bf16[208,1792]{1,0:T(8,128)(2,1)}, bf16[208,1792]{1,0:T(8,128)(2,1)}, u32[]{:S(2)}, u32[]{:S(2)}) collective-permute-start(bf16[208,1792]{1,0:T(8,128)(2,1)} %get-tuple-element.130), channel_id=1, source_target_pairs={{0,16},{4,20},{8,24},{12,28},{16,0},{20,4},{24,8},{28,12},{1,17},{... | collective-permute-start | bytes 2236424 | tf_op jit(solution)/shard_map/ppermute | solution.py:29
  200.2 48.1 %collective-permute-start.16 = (bf16[208,1792]{1,0:T(8,128)(2,1)}, bf16[208,1792]{1,0:T(8,128)(2,1)}, u32[]{:S(2)}, u32[]{:S(2)}) collective-permute-start(bf16[208,1792]{1,0:T(8,128)(2,1)} %get-tuple-element.131), channel_id=1, source_target_pairs={{0,24},{4,28},{8,16},{12,20},{16,8},{20,12},{24,0},{28,4},{1,25},{... | collective-permute-start | bytes 2236424 | tf_op jit(solution)/shard_map/ppermute | solution.py:29
  250.3 14.7 %collective-permute-start.23 = (bf16[208,896]{1,0:T(8,128)(2,1)S(1)}, bf16[208,896]{1,0:T(8,128)(2,1)S(1)}, u32[]{:S(2)}, u32[]{:S(2)}) collective-permute-start(bf16[208,896]{1,0:T(8,128)(2,1)S(1)} %get-tuple-element.163), channel_id=1, source_target_pairs={{0,1},{1,0},{2,3},{3,2},{4,5},{5,4},{6,7},{7,6},{8,9},{9,8},{10,11... | collective-permute-start | bytes 1118216 | tf_op jit(solution)/shard_map/ppermute | solution.py:29
  252.2 14.2 %collective-permute-start.25 = (bf16[208,896]{1,0:T(8,128)(2,1)S(1)}, bf16[208,896]{1,0:T(8,128)(2,1)S(1)}, u32[]{:S(2)}, u32[]{:S(2)}) collective-permute-start(bf16[208,896]{1,0:T(8,128)(2,1)S(1)} %get-tuple-element.155), channel_id=1, source_target_pairs={{2,0},{3,1},{4,6},{5,7},{10,8},{11,9},{12,14},{13,15},{18,16},{19,... | collective-permute-start | bytes 1118216 | tf_op jit(solution)/shard_map/ppermute | solution.py:40
  282.3 20.2 %collective-permute-start.30 = (bf16[208,896]{1,0:T(8,128)(2,1)}, bf16[208,896]{1,0:T(8,128)(2,1)}, u32[]{:S(2)}, u32[]{:S(2)}) collective-permute-start(bf16[208,896]{1,0:T(8,128)(2,1)} %select_select_fusion.refs_0_), channel_id=1, source_target_pairs={{0,8},{4,12},{8,0},{12,4},{16,24},{20,28},{24,16},{28,20},{1,9},{5... | collective-permute-start | bytes 1118216 | tf_op jit(solution)/shard_map/ppermute | solution.py:29
  283.1 19.4 %collective-permute-start.31 = (bf16[208,896]{1,0:T(8,128)(2,1)}, bf16[208,896]{1,0:T(8,128)(2,1)}, u32[]{:S(2)}, u32[]{:S(2)}) collective-permute-start(bf16[208,896]{1,0:T(8,128)(2,1)} %select_select_fusion.refs_0_), channel_id=1, source_target_pairs={{0,16},{4,20},{8,24},{12,28},{16,0},{20,4},{24,8},{28,12},{1,17},{... | collective-permute-start | bytes 1118216 | tf_op jit(solution)/shard_map/ppermute | solution.py:29
  284.6 17.9 %collective-permute-start.32 = (bf16[208,896]{1,0:T(8,128)(2,1)}, bf16[208,896]{1,0:T(8,128)(2,1)}, u32[]{:S(2)}, u32[]{:S(2)}) collective-permute-start(bf16[208,896]{1,0:T(8,128)(2,1)} %select_select_fusion.refs_0_), channel_id=1, source_target_pairs={{0,24},{4,28},{8,16},{12,20},{16,8},{20,12},{24,0},{28,4},{1,25},{... | collective-permute-start | bytes 1118216 | tf_op jit(solution)/shard_map/ppermute | solution.py:29
  287.2 15.3 %collective-permute-start.28 = (f32[56,200]{1,0:T(8,128)S(1)}, f32[56,200]{1,0:T(8,128)S(1)}, u32[]{:S(2)}, u32[]{:S(2)}) collective-permute-start(f32[56,200]{1,0:T(8,128)S(1)} %add.72), channel_id=1, source_target_pairs={{0,8},{4,12},{8,0},{12,4},{16,24},{20,28},{24,16},{28,20},{1,9},{5... | collective-permute-start | bytes 134408 | tf_op jit(solution)/shard_map/ppermute | solution.py:29
  (51 other events, 301.9 us)
